TPU v7x, 32 devices: a whole 2x2x4 slice. The times are simulated.
32 devices in a mesh: kpt: 2 (over core), orb: 16 (over z, y, x).
Axes of the slice: x: 2, y: 2, z: 4, core: 2. Of those that a mesh axis runs over, the one named last changes fastest.
Arguments:
- orbitals: bfloat16 [2, 512, 64, 1024], P('kpt', 'orb'), may hold values from -6 to 6
- potential: float32 [64, 1024], replicated, may hold values from 0.5 to 12
Outputs:
- rotated: bfloat16 [2, 512, 64, 1024], P('kpt', 'orb')
- density: float32 [64, 1024], P('orb')
All inputs are finite; a program needn't handle non-finite values.
Results may differ from a plain program's by a relative error of at most 0.0068.
The roundings to bfloat16 on the way count: a program that leaves them out, or rounds other values in their place, can miss the bound.
Values may be sent and summed in bfloat16 or wider, within the bound.
No kernel may reach another device: no remote copies, remote signals or barrier semaphores. Data moves between devices by JAX's collectives and lax.ppermute only.
A program may use at most 128 MiB of HBM per device.

v0:
```python
import functools
import math

import jax
import jax.numpy as jnp
import numpy as np
from jax import lax
from jax.experimental import pallas as pl
from jax.experimental.pallas import tpu as pltpu
from jax.sharding import PartitionSpec as P

DEG = 4
ITERS = 8
LANES = 128
COLS = 256
CHUNKS = 2
BF = jnp.bfloat16
F32 = jnp.float32

filter_centre = 13.0
filter_half = 9.0
margin_eps = 1e-06


def circulant(taps, first, length):
    matrix = np.zeros((length, length))
    for k in range(len(taps)):
        for i in range(length):
            matrix[i, (i + first + k) % length] += taps[k]
    return matrix


def build_tables(size_x, width):
    side = math.isqrt(width)
    kinetic = [math.pi**2 / 6.0 if k == 0 else (-1.0) ** k / (k * k) for k in range(-14, 15)]
    taps = np.array([math.exp(-((k + 0.5) ** 2) / 6.0) for k in range(-8, 8)])
    taps = taps / taps.sum()
    kin_side = circulant(kinetic, -14, side)
    mag_side = circulant(taps, -8, side)
    kin_yz = np.kron(kin_side, np.eye(side)) + np.kron(np.eye(side), kin_side)
    mag_yz = np.kron(mag_side, mag_side)
    return circulant(kinetic, -14, size_x), circulant(taps, -8, size_x), kin_yz, mag_yz


def to_bf16(table):
    return jnp.asarray(np.asarray(table, np.float32)).astype(BF)


def full_spec(array):
    return pl.BlockSpec(array.shape, lambda *_: (0,) * array.ndim)


def filter_kernel(
    in_ref, pot_ref, kx_ref, mx_ref, kyz_ref, myz_ref, myzt_ref, out_ref,
    now, prev, smooth, mixed, back, nxt, fin, mxt_ref, *, first, firstt,
):
    size_x, width = in_ref.shape[1:]
    rows = now.shape[0]
    group = fin.shape[0] // size_x
    step_id = pl.program_id(0)
    blocks = width // COLS
    span = kx_ref.shape[0]
    tiles = [
        (slice(r, r + span), slice(c, c + COLS))
        for c in range(0, width, COLS)
        for r in range(0, rows, span)
    ]
    dot = functools.partial(jnp.dot, preferred_element_type=F32)
    mxt_ref[...] = mx_ref[...].astype(F32).T.astype(BF)
    start = in_ref[...].reshape(rows, width)
    now[:, :width] = start
    now[:, width:] = start
    prev[...] = start

    def window(src, table, n, lead):
        at = (n + lead) % blocks * COLS
        return dot(src[:, at : at + table.shape[0]], table[...])

    def step(j, carry):
        gain = jnp.where(j == 0, 1.0 / filter_half, 2.0 / filter_half).astype(F32)
        keep = jnp.where(j == 0, 0.0, 1.0).astype(F32)
        for n in range(blocks):
            smooth[:, n * COLS : (n + 1) * COLS] = window(now, myz_ref, n, first).astype(BF)
        for rs, cs in tiles:
            value = dot(mx_ref[...], smooth[rs, cs])
            value = value.reshape(span // size_x, size_x, COLS) * pot_ref[:, cs][None]
            mixed[rs, cs] = value.reshape(span, COLS).astype(BF)
        for rs, cs in tiles:
            value = dot(mxt_ref[...], mixed[rs, cs]).astype(BF)
            back[rs, cs] = value
            back[rs, cs.start + width : cs.stop + width] = value
        for n in range(blocks):
            cs = slice(n * COLS, (n + 1) * COLS)
            total = window(now, kyz_ref, n, 0) + window(back, myzt_ref, n, firstt)
            for r in range(0, rows, span):
                rs = slice(r, r + span)
                value = now[rs, cs]
                shifted = total[rs] + dot(kx_ref[...], value) - filter_centre * value.astype(F32)
                nxt[rs, cs] = (gain * shifted - keep * prev[rs, cs].astype(F32)).astype(BF)
        prev[...] = now[:, :width]
        now[:, :width] = nxt[...]
        now[:, width:] = nxt[...]
        return carry

    lax.fori_loop(0, DEG, step, 0)
    fin[pl.ds(pl.multiple_of(step_id * rows, rows), rows), :] = nxt[...]

    @pl.when(step_id == pl.num_programs(0) - 1)
    def _():
        turned = jnp.swapaxes(fin[...].reshape(group, size_x, width), 0, 1)
        out_ref[...] = turned.reshape(out_ref.shape)


def run_filter(orbitals, chunk, potential, parts, rows):
    size_x, width = orbitals.shape[1:]
    group = orbitals.shape[0] // CHUNKS
    rows = min(rows, group * size_x)
    blocks = width // COLS
    kin_x, mag_x, kin_yz, mag_yz = build_tables(size_x, width)
    span = min(256, rows)
    wide = lambda t: to_bf16(np.kron(np.eye(span // size_x), t))
    piece = lambda t, d: t[:COLS, d % blocks * COLS : (d % blocks + 1) * COLS].T

    def band(t):
        used = [d for d in range(blocks) if np.any(piece(t, d))]
        lead = [d for d in used if (d - 1) % blocks not in used]
        lead = lead[0] if lead else 0
        return lead, to_bf16(np.concatenate([piece(t, lead + i) for i in range(len(used))], 0))

    _, kyz = band(kin_yz)
    first, myz = band(mag_yz)
    firstt, myzt = band(mag_yz.T)
    args = (orbitals, potential, wide(kin_x), wide(mag_x), kyz, myz, myzt)
    per = size_x // parts
    steps = group * size_x // rows
    return pl.pallas_call(
        functools.partial(filter_kernel, first=first, firstt=firstt),
        grid=(steps,),
        in_specs=[
            pl.BlockSpec((rows // size_x, size_x, width), lambda s: (chunk * steps + s, 0, 0))
        ]
        + [full_spec(a) for a in args[1:]],
        out_specs=pl.BlockSpec((parts, per, group, width), lambda s: (0, 0, 0, 0)),
        out_shape=jax.ShapeDtypeStruct((parts, per, group, width), BF),
        scratch_shapes=[
            pltpu.VMEM((rows, 2 * width), BF),
            pltpu.VMEM((rows, width), BF),
            pltpu.VMEM((rows, width), BF),
            pltpu.VMEM((rows, width), BF),
            pltpu.VMEM((rows, 2 * width), BF),
            pltpu.VMEM((rows, width), BF),
            pltpu.VMEM((group * size_x, width), BF),
            pltpu.VMEM((span, span), BF),
        ],
        compiler_params=pltpu.CompilerParams(vmem_limit_bytes=56 << 20),
        cost_estimate=pl.CostEstimate(
            flops=2 * DEG * group * size_x * width
            * (kyz.shape[0] + myz.shape[0] + myzt.shape[0] + 3 * span),
            bytes_accessed=4 * group * size_x * width,
            transcendentals=0,
        ),
        name="chebyshev",
    )(*args)


def triangle(count, side):
    n = count // side
    return [(i, j) for i in range(n) for j in range(i, n)]


def margin_kernel(me_ref, *refs, side, gain, order):
    ins, out_ref, flat, acc = refs[:-3], refs[-3], refs[-2], refs[-1]
    step_id = pl.program_id(0)
    width = flat.shape[1]
    start = 0
    for ref in ins:
        size = ref.shape[0] * ref.shape[2]
        flat[start : start + size, :] = ref[:, 0].reshape(size, width)
        start += size
    n = start // side

    @pl.when(step_id == 0)
    def _():
        acc[...] = jnp.zeros_like(acc)

    at = 0
    for i in range(n):
        got = lax.dot_general(
            flat[i * side : (i + 1) * side, :],
            flat[i * side :, :],
            (((1,), (1,)), ((), ())),
            preferred_element_type=F32,
        )
        for j in range(n - i):
            rs = slice((at + j) * side, (at + j + 1) * side)
            acc[rs, :] += got[:, j * side : (j + 1) * side]
        at += n - i

    @pl.when(step_id == pl.num_programs(0) - 1)
    def _():
        piece = out_ref.shape[1]
        for t, m in enumerate(order):
            rows = pl.multiple_of((me_ref[0] ^ m) * piece, math.gcd(piece, 8))
            out_ref[t] = acc[pl.ds(rows, piece), :] * gain


def run_margin(me, spreads, cells, side, order):
    parts, per, _, width = spreads[0].shape
    count = sum(s.shape[0] * s.shape[2] for s in spreads)
    size = len(triangle(count, side)) * side
    shape = (parts, size // parts, side)
    return pl.pallas_call(
        functools.partial(margin_kernel, side=side, gain=1.0 / cells, order=order),
        grid=(per,),
        in_specs=[pl.BlockSpec(memory_space=pltpu.SMEM)]
        + [pl.BlockSpec((parts, 1, s.shape[2], width), lambda x: (0, x, 0, 0)) for s in spreads],
        out_specs=pl.BlockSpec(shape, lambda x: (0, 0, 0)),
        out_shape=jax.ShapeDtypeStruct(shape, F32),
        scratch_shapes=[pltpu.VMEM((count, width), BF), pltpu.VMEM((size, side), F32)],
        compiler_params=pltpu.CompilerParams(vmem_limit_bytes=48 << 20),
        cost_estimate=pl.CostEstimate(
            flops=count * count * width * per, bytes_accessed=2 * count * width * per,
            transcendentals=0,
        ),
        name="margin",
    )(me, *spreads)


def stage_masks(parts):
    stages, low = [], 1
    while low < parts:
        bits = [low, 2 * low] if 2 * low < parts else [low]
        masks = [0]
        for b in bits:
            masks += [m ^ b for m in masks]
        stages.append(masks)
        low <<= len(bits)
    return stages


def piece_order(stages):
    order = [0]
    for masks in reversed(stages):
        order = [m ^ o for m in masks for o in order]
    return order


def send(value, mask, parts):
    return lax.ppermute(value, "orb", [(i, i ^ mask) for i in range(parts)])


def reduce_margin(held, stages, parts):
    for masks in stages:
        held = held.reshape((len(masks), -1) + held.shape[1:])
        total = held[0]
        for other in [send(held[i], m, parts) for i, m in enumerate(masks) if i]:
            total = total + other
        held = total
    for masks in reversed(stages):
        got = [send(held, m, parts) for m in masks[1:]]
        held = jnp.concatenate([held] + got, axis=0)
    return held


def split(value):
    high = value.astype(BF)
    return high, (value - high.astype(F32)).astype(BF)


def mul(a, b):
    ah, al = a
    bh, bl = b
    dot = functools.partial(jnp.dot, preferred_element_type=F32)
    return dot(ah, bh) + (dot(ah, bl) + dot(al, bh))


def inverse_root_kernel(
    me_ref, held_ref, out_ref, packed, full, pval, zhi, zlo, *, masks, side
):
    me = me_ref[0]
    piece = held_ref.shape[1]
    for t, m in enumerate(masks):
        packed[pl.ds(pl.multiple_of((me ^ m) * piece, math.gcd(piece, 8)), piece), :] = held_ref[t]
    count = full.shape[0]
    for at, (i, j) in enumerate(triangle(count, side)):
        tile = packed[at * side : (at + 1) * side, :]
        full[i * side : (i + 1) * side, j * side : (j + 1) * side] = tile
        if i != j:
            full[j * side : (j + 1) * side, i * side : (i + 1) * side] = tile.T
    margin = full[...]
    total = jnp.sum(jnp.sum(margin * margin, axis=1, keepdims=True), axis=0, keepdims=True)
    scale = jnp.sqrt(total + margin_eps)
    row = lax.broadcasted_iota(jnp.int32, (count, count), 0)
    col = lax.broadcasted_iota(jnp.int32, (count, count), 1)
    eye = jnp.where(row == col, 1.0, 0.0).astype(F32)

    def factor(ps, p):
        square = mul(ps, ps)
        inner = 6.75 * eye - 2.25 * p + 0.25 * square
        return 0.25 * (9.0 * eye - 9.75 * p + mul(split(square), split(inner)))

    def pair(p, last):
        ps = split(p)
        ws = split(factor(ps, p))
        return ws, None if last else mul(ws, split(mul(ws, ps)))

    ws, pval[...] = pair(margin / scale, False)
    zhi[...], zlo[...] = ws

    def middle(_, carry):
        ws, pval[...] = pair(pval[...], False)
        zhi[...], zlo[...] = split(mul(ws, (zhi[...], zlo[...])))
        return carry

    lax.fori_loop(0, ITERS // 2 - 2, middle, 0)
    ws, _ = pair(pval[...], True)
    z = mul(ws, (zhi[...], zlo[...]))
    out_ref[...] = (z / jnp.sqrt(scale)).astype(BF)


def run_inverse_root(me, held, masks, count, side):
    return pl.pallas_call(
        functools.partial(inverse_root_kernel, masks=masks, side=side),
        in_specs=[
            pl.BlockSpec(memory_space=pltpu.SMEM),
            pl.BlockSpec(memory_space=pltpu.VMEM),
        ],
        out_specs=pl.BlockSpec(memory_space=pltpu.VMEM),
        out_shape=jax.ShapeDtypeStruct((count, count), BF),
        scratch_shapes=[
            pltpu.VMEM((held.shape[0] * held.shape[1], side), F32),
            pltpu.VMEM((count, count), F32),
            pltpu.VMEM((count, count), F32),
            pltpu.VMEM((count, count), BF),
            pltpu.VMEM((count, count), BF),
        ],
        compiler_params=pltpu.CompilerParams(vmem_limit_bytes=48 << 20),
        cost_estimate=pl.CostEstimate(
            flops=2 * 51 * count**3, bytes_accessed=4 * count * count, transcendentals=0
        ),
        name="inverse_root",
    )(me, held)


def rotate_kernel(*refs):
    coeff_ref, ins, out_ref, den_ref, flat = refs[0], refs[1:-3], refs[-3], refs[-2], refs[-1]
    width = flat.shape[1]
    start = 0
    for ref in ins:
        size = ref.shape[0] * ref.shape[2]
        flat[start : start + size, :] = ref[:, 0].reshape(size, width)
        start += size
    value = jnp.dot(coeff_ref[...], flat[...], preferred_element_type=F32).astype(BF)
    out_ref[:, 0] = value.reshape(out_ref.shape[0], out_ref.shape[2], width)
    wide = value.astype(F32)
    den_ref[...] = jnp.sum(wide * wide, axis=0)[None, None]


def run_rotate(coeff, spreads):
    parts, per, group, width = spreads[0].shape
    count = coeff.shape[1]
    return pl.pallas_call(
        rotate_kernel,
        grid=(per,),
        in_specs=[full_spec(coeff)]
        + [pl.BlockSpec((parts, 1, s.shape[2], width), lambda x: (0, x, 0, 0)) for s in spreads],
        out_specs=[
            pl.BlockSpec((parts, 1, group, width), lambda x: (0, x, 0, 0)),
            pl.BlockSpec((1, 1, width), lambda x: (x, 0, 0)),
        ],
        out_shape=[
            jax.ShapeDtypeStruct((parts, per, group, width), BF),
            jax.ShapeDtypeStruct((per, 1, width), F32),
        ],
        scratch_shapes=[pltpu.VMEM((count, width), BF)],
        compiler_params=pltpu.CompilerParams(vmem_limit_bytes=48 << 20),
        cost_estimate=pl.CostEstimate(
            flops=2 * count * parts * group * width * per,
            bytes_accessed=2 * (count + parts * group) * width * per,
            transcendentals=0,
        ),
        name="rotate",
    )(coeff, *spreads)


def restore_kernel(*refs):
    in_ref, out_ref, wide = refs[0], refs[-2], refs[-1]
    parts, per, group, _ = in_ref.shape
    for s in range(parts):
        for x in range(per):
            wide[pl.ds((s * per + x) * group, group), :] = in_ref[s, x].astype(F32)
    for g in range(group):
        out_ref[g] = wide[pl.ds(g, parts * per, stride=group), :].astype(BF)


def run_restore(spread, target, chunk, chunks):
    parts, per, group, width = spread.shape
    size_x = parts * per
    args = (spread,) if target is None else (spread, target)
    return pl.pallas_call(
        restore_kernel,
        grid=(width // LANES,),
        in_specs=[pl.BlockSpec((parts, per, group, LANES), lambda l: (0, 0, 0, l))]
        + [pl.BlockSpec(memory_space=pl.ANY)] * (len(args) - 1),
        out_specs=pl.BlockSpec((group, size_x, LANES), lambda l: (chunk, 0, l)),
        out_shape=jax.ShapeDtypeStruct((group * chunks, size_x, width), BF),
        scratch_shapes=[pltpu.VMEM((size_x * group, LANES), F32)],
        input_output_aliases={} if target is None else {1: 0},
        cost_estimate=pl.CostEstimate(
            flops=0, bytes_accessed=4 * group * size_x * width, transcendentals=0
        ),
        name="restore",
    )(*args)


def shards(orbitals, potential):
    parts = lax.axis_size("orb")
    mine, size_x, width = orbitals.shape[1:]
    group = mine // CHUNKS
    count = mine * parts
    exchange = lambda v: lax.all_to_all(v, "orb", split_axis=0, concat_axis=0, tiled=True)
    spreads = []
    for c in range(CHUNKS):
        spreads.append(exchange(run_filter(orbitals[0], c, potential, parts, 512)))
    me = lax.axis_index("orb").astype(jnp.int32).reshape(1)
    stages = stage_masks(parts)
    order = piece_order(stages)
    partial = run_margin(me, spreads, size_x * width, LANES, order)
    held = reduce_margin(partial, stages, parts)
    coeff = run_inverse_root(me, held, order, count, LANES)
    own = group * parts
    target = None
    density = 0.0
    returned = []
    for c in range(CHUNKS):
        rotated, part = run_rotate(coeff[c * own : (c + 1) * own], spreads)
        returned.append(exchange(rotated))
        density = density + part[:, 0]
    for c in range(CHUNKS):
        target = run_restore(returned[c], target, c, CHUNKS)
    kpoints = lax.axis_size("kpt")
    total = density
    for k in range(1, kpoints):
        total = total + lax.ppermute(
            density, "kpt", [(i, (i + k) % kpoints) for i in range(kpoints)]
        )
    weight = 1.0 / (kpoints * math.sqrt(count))
    return target[None], total * weight


def solution(mesh):
    in_specs = (P("kpt", "orb", None, None), P())
    out_specs = (P("kpt", "orb", None, None), P("orb", None))
    return jax.shard_map(shards, mesh=mesh, in_specs=in_specs, out_specs=out_specs, check_vma=False)
```

profile of v0, /device:TPU:12, one launch (start us, length us, event | category | flops | bytes accessed | tf_op | source)
XLA Modules:
  0.0 314.1 jit_solution(1860094236191591535)
XLA Ops:
  0.6 36.5 %chebyshev.3 = bf16[16,4,16,1024]{3,2,1,0:T(8,128)(2,1)} custom-call(bf16[32,64,1024]{2,1,0:T(8,128)(2,1)} %bitcast.10, f32[64,1024]{1,0:T(8,128)} %pot_ref.3, bf16[256,256]{1,0:T(8,128)(2,1)} %constant.22.kx_ref, bf16[256,256]{1,0:T(8,128)(2,1)} %constant.23.mx_ref, bf16[1024,256]{1,0:T(8,128)(2,1)} %constant.24.kyz_ref, ...), custom_call_target="tpu_custom_call" | custom-call | flops 27917287424 | bytes 4194304 | tf_op jit(solution)/shard_map/chebyshev/pallas_call | solution.py:136
  37.1 7.2 %all-to-all-start.1 = ((bf16[16,4,16,1024]{3,2,1,0:T(8,128)(2,1)}), bf16[16,4,16,1024]{3,2,1,0:T(8,128)(2,1)S(1)}, u32[]{:S(2)}, u32[]{:S(2)}) async-start(bf16[16,4,16,1024]{3,2,1,0:T(8,128)(2,1)} %chebyshev.3), calls=%async_computation.1 | async-start | bytes 4194304 | tf_op jit(solution)/shard_map/all_to_all | solution.py:421
  44.3 36.5 %chebyshev.2 = bf16[16,4,16,1024]{3,2,1,0:T(8,128)(2,1)} custom-call(bf16[32,64,1024]{2,1,0:T(8,128)(2,1)} %bitcast.11, f32[64,1024]{1,0:T(8,128)} %pot_ref.3, bf16[256,256]{1,0:T(8,128)(2,1)} %constant.22.kx_ref, bf16[256,256]{1,0:T(8,128)(2,1)} %constant.23.mx_ref, bf16[1024,256]{1,0:T(8,128)(2,1)} %constant.24.kyz_ref, ...), custom_call_target="tpu_custom_call" | custom-call | flops 27917287424 | bytes 4194304 | tf_op jit(solution)/shard_map/chebyshev/pallas_call | solution.py:136
  80.8 11.7 %all-to-all-done.1.refs_1_.refs_2_ = bf16[16,4,16,1024]{3,2,1,0:T(8,128)(2,1)S(1)} async-done(((bf16[16,4,16,1024]{3,2,1,0:T(8,128)(2,1)}), bf16[16,4,16,1024]{3,2,1,0:T(8,128)(2,1)S(1)}, u32[]{:S(2)}, u32[]{:S(2)}) %all-to-all-start.1) | async-done | bytes 2097184 | tf_op jit(solution)/shard_map/all_to_all | solution.py:421
  92.5 4.9 %all-to-all-start = ((bf16[16,4,16,1024]{3,2,1,0:T(8,128)(2,1)}), bf16[16,4,16,1024]{3,2,1,0:T(8,128)(2,1)}, u32[]{:S(2)}, u32[]{:S(2)}) async-start(bf16[16,4,16,1024]{3,2,1,0:T(8,128)(2,1)} %chebyshev.2), calls=%async_computation | async-start | bytes 4194304 | tf_op jit(solution)/shard_map/all_to_all | solution.py:421
  97.4 47.8 %all-to-all-done.refs_0_.refs_1_ = bf16[16,4,16,1024]{3,2,1,0:T(8,128)(2,1)} async-done(((bf16[16,4,16,1024]{3,2,1,0:T(8,128)(2,1)}), bf16[16,4,16,1024]{3,2,1,0:T(8,128)(2,1)}, u32[]{:S(2)}, u32[]{:S(2)}) %all-to-all-start) | async-done | bytes 2097184 | tf_op jit(solution)/shard_map/all_to_all | solution.py:421
  145.1 5.3 %margin.1 = f32[16,80,128]{2,1,0:T(8,128)S(1)} custom-call(s32[1]{0:T(128)} %bitcast.me_ref, bf16[16,4,16,1024]{3,2,1,0:T(8,128)(2,1)} %all-to-all-done.refs_0_.refs_1_, bf16[16,4,16,1024]{3,2,1,0:T(8,128)(2,1)S(1)} %all-to-all-done.1.refs_1_.refs_2_), custom_call_target="tpu_custom_call" | custom-call | flops 1073741824 | bytes 4194304 | tf_op jit(solution)/shard_map/margin/pallas_call | solution.py:212
  150.5 0.9 collective-permute-start
  151.7 2.4 collective-permute-start.1
  154.1 3.5 %collective-permute-done = f32[4,80,128]{2,1,0:T(8,128)S(1)} collective-permute-done((f32[4,80,128]{2,1,0:T(8,128)S(1)}, f32[4,80,128]{2,1,0:T(8,128)S(1)}, u32[]{:S(2)}, u32[]{:S(2)}) %collective-permute-start) | collective-permute-done | bytes 163872 | tf_op jit(solution)/shard_map/ppermute | solution.py:249
  157.6 1.0 collective-permute-done.2
  158.6 1.9 collective-permute-done.1
  161.2 3.8 %collective-permute-start.4 = (f32[1,80,128]{2,1,0:T(8,128)S(1)}, f32[1,80,128]{2,1,0:T(8,128)S(1)}, u32[]{:S(2)}, u32[]{:S(2)}) collective-permute-start(f32[1,80,128]{2,1,0:T(8,128)S(1)} %get-tuple-element.19), channel_id=1, source_target_pairs={{0,8},{1,9},{2,10},{3,11},{4,12},{5,13},{6,14},{7,15},{8,0},{9,1},... | collective-permute-start | bytes 122888 | tf_op jit(solution)/shard_map/ppermute | solution.py:249
  165.6 1.9 collective-permute-done.4
  168.0 3.8 %collective-permute-start.7 = (f32[1,80,128]{2,1,0:T(8,128)S(1)}, f32[1,80,128]{2,1,0:T(8,128)S(1)}, u32[]{:S(2)}, u32[]{:S(2)}) collective-permute-start(f32[1,80,128]{2,1,0:T(8,128)S(1)} %get-tuple-element.11), channel_id=1, source_target_pairs={{0,8},{1,9},{2,10},{3,11},{4,12},{5,13},{6,14},{7,15},{8,0},{9,1},... | collective-permute-start | bytes 122888 | tf_op jit(solution)/shard_map/ppermute | solution.py:249
  171.8 2.4 collective-permute-done.7
  174.2 1.6 collective-permute-done.6
  175.8 1.2 collective-permute-start.11
  177.0 1.2 collective-permute-start.10
  178.2 1.2 collective-permute-start.9
  179.4 4.1 %collective-permute-done.9 = f32[4,80,128]{2,1,0:T(8,128)S(1)} collective-permute-done((f32[4,80,128]{2,1,0:T(8,128)S(1)}, f32[4,80,128]{2,1,0:T(8,128)S(1)}, u32[]{:S(2)}, u32[]{:S(2)}) %collective-permute-start.9) | collective-permute-done | bytes 163872 | tf_op jit(solution)/shard_map/ppermute | solution.py:249
  183.9 16.1 %inverse_root.1 = bf16[512,512]{1,0:T(8,128)(2,1)S(1)} custom-call(s32[1]{0:T(128)} %bitcast.me_ref, f32[16,80,128]{2,1,0:T(8,128)S(1)} %constant_dynamic-update-slice_fusion.held_ref), custom_call_target="tpu_custom_call" | custom-call | flops 13690208256 | bytes 1048576 | tf_op jit(solution)/shard_map/inverse_root/pallas_call | solution.py:322
  200.1 5.0 %rotate.3 = (bf16[16,4,16,1024]{3,2,1,0:T(8,128)(2,1)}, f32[4,1,1024]{2,1,0:T(1,128)S(1)}) custom-call(bf16[256,512]{1,0:T(8,128)(2,1)S(1)} %get-tuple-element.15.refs_0_, bf16[16,4,16,1024]{3,2,1,0:T(8,128)(2,1)} %all-to-all-done.refs_0_.refs_1_, bf16[16,4,16,1024]{3,2,1,0:T(8,128)(2,1)} %copy-done), custom_call_target="tpu_custom_call" | custom-call | flops 1073741824 | bytes 6291456 | tf_op jit(solution)/shard_map/rotate/pallas_call | solution.py:362
  205.1 5.4 %all-to-all-start.3 = ((bf16[16,4,16,1024]{3,2,1,0:T(8,128)(2,1)}), bf16[16,4,16,1024]{3,2,1,0:T(8,128)(2,1)S(1)}, u32[]{:S(2)}, u32[]{:S(2)}) async-start(bf16[16,4,16,1024]{3,2,1,0:T(8,128)(2,1)} %get-tuple-element.7), calls=%async_computation.3 | async-start | bytes 4194304 | tf_op jit(solution)/shard_map/all_to_all | solution.py:421
  210.5 5.1 %rotate.2 = (bf16[16,4,16,1024]{3,2,1,0:T(8,128)(2,1)}, f32[4,1,1024]{2,1,0:T(1,128)S(1)}) custom-call(bf16[256,512]{1,0:T(8,128)(2,1)S(1)} %get-tuple-element.16.refs_0_, bf16[16,4,16,1024]{3,2,1,0:T(8,128)(2,1)} %all-to-all-done.refs_0_.refs_1_, bf16[16,4,16,1024]{3,2,1,0:T(8,128)(2,1)} %copy-done), custom_call_target="tpu_custom_call" | custom-call | flops 1073741824 | bytes 6291456 | tf_op jit(solution)/shard_map/rotate/pallas_call | solution.py:362
  215.6 38.3 %all-to-all-done.3.refs_0_ = bf16[16,4,16,1024]{3,2,1,0:T(8,128)(2,1)S(1)} async-done(((bf16[16,4,16,1024]{3,2,1,0:T(8,128)(2,1)}), bf16[16,4,16,1024]{3,2,1,0:T(8,128)(2,1)S(1)}, u32[]{:S(2)}, u32[]{:S(2)}) %all-to-all-start.3) | async-done | bytes 2097184 | tf_op jit(solution)/shard_map/all_to_all | solution.py:421
  253.9 1.3 copy-done.1
  255.2 4.9 %all-to-all-start.2 = ((bf16[16,4,16,1024]{3,2,1,0:T(8,128)(2,1)}), bf16[16,4,16,1024]{3,2,1,0:T(8,128)(2,1)}, u32[]{:S(2)}, u32[]{:S(2)}) async-start(bf16[16,4,16,1024]{3,2,1,0:T(8,128)(2,1)} %get-tuple-element.6), calls=%async_computation.2 | async-start | bytes 4194304 | tf_op jit(solution)/shard_map/all_to_all | solution.py:421
  260.3 1.2 collective-permute-done.12
  262.0 6.2 %restore.2.refs_1_ = bf16[32,64,1024]{2,1,0:T(8,128)(2,1)} custom-call(bf16[16,4,16,1024]{3,2,1,0:T(8,128)(2,1)} %copy-done.1), custom_call_target="tpu_custom_call" | custom-call | bytes 4194304 | tf_op jit(solution)/shard_map/restore/pallas_call | solution.py:400
  268.3 39.6 %all-to-all-done.2.refs_0_ = bf16[16,4,16,1024]{3,2,1,0:T(8,128)(2,1)} async-done(((bf16[16,4,16,1024]{3,2,1,0:T(8,128)(2,1)}), bf16[16,4,16,1024]{3,2,1,0:T(8,128)(2,1)}, u32[]{:S(2)}, u32[]{:S(2)}) %all-to-all-start.2) | async-done | bytes 2097184 | tf_op jit(solution)/shard_map/all_to_all | solution.py:421
  307.8 6.2 %restore.3 = bf16[32,64,1024]{2,1,0:T(8,128)(2,1)} custom-call(bf16[16,4,16,1024]{3,2,1,0:T(8,128)(2,1)} %all-to-all-done.2.refs_0_, bf16[32,64,1024]{2,1,0:T(8,128)(2,1)} %restore.2.refs_1_), custom_call_target="tpu_custom_call", output_to_operand_aliasing={{}: (1, {})} | custom-call | bytes 4194304 | tf_op jit(solution)/shard_map/restore/pallas_call | solution.py:400
  (29 shorter events, 3.1 us)
Async XLA Ops:
  37.1 55.3 %all-to-all-start.1 = ((bf16[16,4,16,1024]{3,2,1,0:T(8,128)(2,1)}), bf16[16,4,16,1024]{3,2,1,0:T(8,128)(2,1)S(1)}, u32[]{:S(2)}, u32[]{:S(2)}) async-start(bf16[16,4,16,1024]{3,2,1,0:T(8,128)(2,1)} %chebyshev.3), calls=%async_computation.1 | async-start | bytes 4194304 | tf_op jit(solution)/shard_map/all_to_all | solution.py:421
  92.5 52.7 %copy-start = (bf16[16,4,16,1024]{3,2,1,0:T(8,128)(2,1)}, bf16[16,4,16,1024]{3,2,1,0:T(8,128)(2,1)S(1)}, u32[]{:S(2)}) copy-start(bf16[16,4,16,1024]{3,2,1,0:T(8,128)(2,1)S(1)} %all-to-all-done.1.refs_1_.refs_2_) | copy-start | bytes 6291460
  92.5 52.7 %all-to-all-start = ((bf16[16,4,16,1024]{3,2,1,0:T(8,128)(2,1)}), bf16[16,4,16,1024]{3,2,1,0:T(8,128)(2,1)}, u32[]{:S(2)}, u32[]{:S(2)}) async-start(bf16[16,4,16,1024]{3,2,1,0:T(8,128)(2,1)} %chebyshev.2), calls=%async_computation | async-start | bytes 4194304 | tf_op jit(solution)/shard_map/all_to_all | solution.py:421
  150.5 7.0 %collective-permute-start = (f32[4,80,128]{2,1,0:T(8,128)S(1)}, f32[4,80,128]{2,1,0:T(8,128)S(1)}, u32[]{:S(2)}, u32[]{:S(2)}) collective-permute-start(f32[4,80,128]{2,1,0:T(8,128)S(1)} %get-tuple-element.12), channel_id=1, source_target_pairs={{0,1},{1,0},{2,3},{3,2},{4,5},{5,4},{6,7},{7,6},{8,9},{9,8},{10,11... | collective-permute-start | bytes 491528 | tf_op jit(solution)/shard_map/ppermute | solution.py:249
  151.5 7.2 %collective-permute-start.2 = (f32[4,80,128]{2,1,0:T(8,128)S(1)}, f32[4,80,128]{2,1,0:T(8,128)S(1)}, u32[]{:S(2)}, u32[]{:S(2)}) collective-permute-start(f32[4,80,128]{2,1,0:T(8,128)S(1)} %get-tuple-element.13), channel_id=1, source_target_pairs={{0,3},{1,2},{2,1},{3,0},{4,7},{5,6},{6,5},{7,4},{8,11},{9,10},{10,... | collective-permute-start | bytes 491528 | tf_op jit(solution)/shard_map/ppermute | solution.py:249
  151.7 8.8 %collective-permute-start.1 = (f32[4,80,128]{2,1,0:T(8,128)S(1)}, f32[4,80,128]{2,1,0:T(8,128)S(1)}, u32[]{:S(2)}, u32[]{:S(2)}) collective-permute-start(f32[4,80,128]{2,1,0:T(8,128)S(1)} %get-tuple-element.14), channel_id=1, source_target_pairs={{0,2},{1,3},{2,0},{3,1},{4,6},{5,7},{6,4},{7,5},{8,10},{9,11},{10,... | collective-permute-start | bytes 491528 | tf_op jit(solution)/shard_map/ppermute | solution.py:249
  160.6 4.5 %collective-permute-start.3 = (f32[1,80,128]{2,1,0:T(8,128)S(1)}, f32[1,80,128]{2,1,0:T(8,128)S(1)}, u32[]{:S(2)}, u32[]{:S(2)}) collective-permute-start(f32[1,80,128]{2,1,0:T(8,128)S(1)} %get-tuple-element.17), channel_id=1, source_target_pairs={{0,4},{1,5},{2,6},{3,7},{4,0},{5,1},{6,2},{7,3},{8,12},{9,13},{10,... | collective-permute-start | bytes 122888 | tf_op jit(solution)/shard_map/ppermute | solution.py:249
  160.7 4.9 %collective-permute-start.5 = (f32[1,80,128]{2,1,0:T(8,128)S(1)}, f32[1,80,128]{2,1,0:T(8,128)S(1)}, u32[]{:S(2)}, u32[]{:S(2)}) collective-permute-start(f32[1,80,128]{2,1,0:T(8,128)S(1)} %get-tuple-element.18), channel_id=1, source_target_pairs={{0,12},{1,13},{2,14},{3,15},{4,8},{5,9},{6,10},{7,11},{8,4},{9,5},... | collective-permute-start | bytes 122888 | tf_op jit(solution)/shard_map/ppermute | solution.py:249
  161.2 6.3 %collective-permute-start.4 = (f32[1,80,128]{2,1,0:T(8,128)S(1)}, f32[1,80,128]{2,1,0:T(8,128)S(1)}, u32[]{:S(2)}, u32[]{:S(2)}) collective-permute-start(f32[1,80,128]{2,1,0:T(8,128)S(1)} %get-tuple-element.19), channel_id=1, source_target_pairs={{0,8},{1,9},{2,10},{3,11},{4,12},{5,13},{6,14},{7,15},{8,0},{9,1},... | collective-permute-start | bytes 122888 | tf_op jit(solution)/shard_map/ppermute | solution.py:249
  167.5 4.3 %collective-permute-start.8 = (f32[1,80,128]{2,1,0:T(8,128)S(1)}, f32[1,80,128]{2,1,0:T(8,128)S(1)}, u32[]{:S(2)}, u32[]{:S(2)}) collective-permute-start(f32[1,80,128]{2,1,0:T(8,128)S(1)} %get-tuple-element.11), channel_id=1, source_target_pairs={{0,12},{1,13},{2,14},{3,15},{4,8},{5,9},{6,10},{7,11},{8,4},{9,5},... | collective-permute-start | bytes 122888 | tf_op jit(solution)/shard_map/ppermute | solution.py:249
  168.0 6.2 %collective-permute-start.7 = (f32[1,80,128]{2,1,0:T(8,128)S(1)}, f32[1,80,128]{2,1,0:T(8,128)S(1)}, u32[]{:S(2)}, u32[]{:S(2)}) collective-permute-start(f32[1,80,128]{2,1,0:T(8,128)S(1)} %get-tuple-element.11), channel_id=1, source_target_pairs={{0,8},{1,9},{2,10},{3,11},{4,12},{5,13},{6,14},{7,15},{8,0},{9,1},... | collective-permute-start | bytes 122888 | tf_op jit(solution)/shard_map/ppermute | solution.py:249
  171.8 4.0 %collective-permute-start.6 = (f32[1,80,128]{2,1,0:T(8,128)S(1)}, f32[1,80,128]{2,1,0:T(8,128)S(1)}, u32[]{:S(2)}, u32[]{:S(2)}) collective-permute-start(f32[1,80,128]{2,1,0:T(8,128)S(1)} %get-tuple-element.11), channel_id=1, source_target_pairs={{0,4},{1,5},{2,6},{3,7},{4,0},{5,1},{6,2},{7,3},{8,12},{9,13},{10,... | collective-permute-start | bytes 122888 | tf_op jit(solution)/shard_map/ppermute | solution.py:249
  175.8 8.1 %collective-permute-start.11 = (f32[4,80,128]{2,1,0:T(8,128)S(1)}, f32[4,80,128]{2,1,0:T(8,128)S(1)}, u32[]{:S(2)}, u32[]{:S(2)}) collective-permute-start(f32[4,80,128]{2,1,0:T(8,128)S(1)} %pad_maximum_fusion), channel_id=1, source_target_pairs={{0,3},{1,2},{2,1},{3,0},{4,7},{5,6},{6,5},{7,4},{8,11},{9,10},{10,... | collective-permute-start | bytes 491528 | tf_op jit(solution)/shard_map/ppermute | solution.py:249
  177.0 6.8 %collective-permute-start.10 = (f32[4,80,128]{2,1,0:T(8,128)S(1)}, f32[4,80,128]{2,1,0:T(8,128)S(1)}, u32[]{:S(2)}, u32[]{:S(2)}) collective-permute-start(f32[4,80,128]{2,1,0:T(8,128)S(1)} %pad_maximum_fusion), channel_id=1, source_target_pairs={{0,2},{1,3},{2,0},{3,1},{4,6},{5,7},{6,4},{7,5},{8,10},{9,11},{10,... | collective-permute-start | bytes 491528 | tf_op jit(solution)/shard_map/ppermute | solution.py:249
  178.2 5.3 %collective-permute-start.9 = (f32[4,80,128]{2,1,0:T(8,128)S(1)}, f32[4,80,128]{2,1,0:T(8,128)S(1)}, u32[]{:S(2)}, u32[]{:S(2)}) collective-permute-start(f32[4,80,128]{2,1,0:T(8,128)S(1)} %pad_maximum_fusion), channel_id=1, source_target_pairs={{0,1},{1,0},{2,3},{3,2},{4,5},{5,4},{6,7},{7,6},{8,9},{9,8},{10,11... | collective-permute-start | bytes 491528 | tf_op jit(solution)/shard_map/ppermute | solution.py:249
  205.1 48.8 %all-to-all-start.3 = ((bf16[16,4,16,1024]{3,2,1,0:T(8,128)(2,1)}), bf16[16,4,16,1024]{3,2,1,0:T(8,128)(2,1)S(1)}, u32[]{:S(2)}, u32[]{:S(2)}) async-start(bf16[16,4,16,1024]{3,2,1,0:T(8,128)(2,1)} %get-tuple-element.7), calls=%async_computation.3 | async-start | bytes 4194304 | tf_op jit(solution)/shard_map/all_to_all | solution.py:421
  253.9 1.4 copy-start.1
  255.2 52.6 %all-to-all-start.2 = ((bf16[16,4,16,1024]{3,2,1,0:T(8,128)(2,1)}), bf16[16,4,16,1024]{3,2,1,0:T(8,128)(2,1)}, u32[]{:S(2)}, u32[]{:S(2)}) async-start(bf16[16,4,16,1024]{3,2,1,0:T(8,128)(2,1)} %get-tuple-element.6), calls=%async_computation.2 | async-start | bytes 4194304 | tf_op jit(solution)/shard_map/all_to_all | solution.py:421
  260.2 1.2 collective-permute-start.12
where the time goes:
time: 315 us; the launch traced here: 314 us
  waiting for transfers between devices  156 us (50%)
  Pallas kernels  117 us (37%)
  starting transfers between devices  38.3 us (12%)
    all_to_all x4, waiting for transfers between devices, shards(): lax.all_to_all(v, 'orb', split_axis=0, concat_axis=0, tiled=True)  137 us
    pallas_call x2, Pallas kernels, run_filter(): pl.pallas_call(functools.partial(filter_kernel, first=first, firstt=first...  73 us
    all_to_all x4, starting transfers between devices, shards(): lax.all_to_all(v, 'orb', split_axis=0, concat_axis=0, tiled=True)  22.4 us
    ppermute x12, waiting for transfers between devices, send(): return lax.ppermute(value, 'orb', [(i, i ^ mask) for i in range(parts)])  17.3 us
    pallas_call x1, Pallas kernels, run_inverse_root(): pl.pallas_call(functools.partial(inverse_root_kernel, masks=masks, side=s...  16.1 us
    ppermute x12, starting transfers between devices, send(): return lax.ppermute(value, 'orb', [(i, i ^ mask) for i in range(parts)])  15.8 us
    pallas_call x2, Pallas kernels, run_restore(): pl.pallas_call(restore_kernel, grid=(width // LANES,), in_specs=[pl.Block...  12.5 us
    pallas_call x2, Pallas kernels, run_rotate(): pl.pallas_call(rotate_kernel, grid=(per,), in_specs=[full_spec(coeff)] +...  10.1 us
  transfers between devices with their start and end apart: 17, of which 14 were waited for; matrix products, arithmetic and copies ran while one was open for 0% of the time, Pallas kernels for 15%

commit v1 on v0

--- a/solution.py
+++ b/solution.py
@@ -13,7 +13,7 @@
 ITERS = 8
 LANES = 128
 COLS = 256
-CHUNKS = 2
+OUT_CHUNKS = 2
 BF = jnp.bfloat16
 F32 = jnp.float32
 
@@ -111,9 +111,9 @@
         out_ref[...] = turned.reshape(out_ref.shape)
 
 
-def run_filter(orbitals, chunk, potential, parts, rows):
+def run_filter(orbitals, chunk, chunks, potential, parts, rows):
     size_x, width = orbitals.shape[1:]
-    group = orbitals.shape[0] // CHUNKS
+    group = orbitals.shape[0] // chunks
     rows = min(rows, group * size_x)
     blocks = width // COLS
     kin_x, mag_x, kin_yz, mag_yz = build_tables(size_x, width)
@@ -168,33 +168,36 @@
     return [(i, j) for i in range(n) for j in range(i, n)]
 
 
-def margin_kernel(me_ref, *refs, side, gain, order):
-    ins, out_ref, flat, acc = refs[:-3], refs[-3], refs[-2], refs[-1]
-    step_id = pl.program_id(0)
-    width = flat.shape[1]
+def gather_rows(ins, flat):
     start = 0
     for ref in ins:
         size = ref.shape[0] * ref.shape[2]
-        flat[start : start + size, :] = ref[:, 0].reshape(size, width)
+        flat[start : start + size, :] = (
+            ref[:, 0].astype(F32).reshape(size, flat.shape[1]).astype(BF)
+        )
         start += size
-    n = start // side
+
+
+def margin_kernel(me_ref, *refs, side, gain, order, blocks, sources):
+    ins, out_ref, flat, acc = refs[:sources], refs[-3], refs[-2], refs[-1]
+    step_id = pl.program_id(0)
+    gather_rows(ins, flat)
 
     @pl.when(step_id == 0)
     def _():
         acc[...] = jnp.zeros_like(acc)
 
-    at = 0
-    for i in range(n):
+    for i in sorted({i for i, _ in blocks}):
+        cols = [j for b, j in blocks if b == i]
         got = lax.dot_general(
             flat[i * side : (i + 1) * side, :],
-            flat[i * side :, :],
+            flat[cols[0] * side : (cols[-1] + 1) * side, :],
             (((1,), (1,)), ((), ())),
             preferred_element_type=F32,
         )
-        for j in range(n - i):
-            rs = slice((at + j) * side, (at + j + 1) * side)
-            acc[rs, :] += got[:, j * side : (j + 1) * side]
-        at += n - i
+        for at, j in enumerate(cols):
+            row = blocks.index((i, j)) * side
+            acc[row : row + side, :] += got[:, at * side : (at + 1) * side]
 
     @pl.when(step_id == pl.num_programs(0) - 1)
     def _():
@@ -204,26 +207,30 @@
             out_ref[t] = acc[pl.ds(rows, piece), :] * gain
 
 
-def run_margin(me, spreads, cells, side, order):
+def run_margin(me, spreads, cells, side, order, blocks, after):
     parts, per, _, width = spreads[0].shape
     count = sum(s.shape[0] * s.shape[2] for s in spreads)
-    size = len(triangle(count, side)) * side
+    size = len(blocks) * side
     shape = (parts, size // parts, side)
     return pl.pallas_call(
-        functools.partial(margin_kernel, side=side, gain=1.0 / cells, order=order),
+        functools.partial(
+            margin_kernel, side=side, gain=1.0 / cells, order=order, blocks=blocks,
+            sources=len(spreads),
+        ),
         grid=(per,),
         in_specs=[pl.BlockSpec(memory_space=pltpu.SMEM)]
-        + [pl.BlockSpec((parts, 1, s.shape[2], width), lambda x: (0, x, 0, 0)) for s in spreads],
+        + [pl.BlockSpec((parts, 1, s.shape[2], width), lambda x: (0, x, 0, 0)) for s in spreads]
+        + [pl.BlockSpec(memory_space=pl.ANY)] * len(after),
         out_specs=pl.BlockSpec(shape, lambda x: (0, 0, 0)),
         out_shape=jax.ShapeDtypeStruct(shape, F32),
         scratch_shapes=[pltpu.VMEM((count, width), BF), pltpu.VMEM((size, side), F32)],
         compiler_params=pltpu.CompilerParams(vmem_limit_bytes=48 << 20),
         cost_estimate=pl.CostEstimate(
-            flops=count * count * width * per, bytes_accessed=2 * count * width * per,
+            flops=2 * size * side * width * per, bytes_accessed=2 * count * width * per,
             transcendentals=0,
         ),
         name="margin",
-    )(me, *spreads)
+    )(me, *spreads, *after)
 
 
 def stage_masks(parts):
@@ -249,13 +256,17 @@
     return lax.ppermute(value, "orb", [(i, i ^ mask) for i in range(parts)])
 
 
-def reduce_margin(held, stages, parts):
+def scatter_sum(held, stages, parts):
     for masks in stages:
         held = held.reshape((len(masks), -1) + held.shape[1:])
         total = held[0]
         for other in [send(held[i], m, parts) for i, m in enumerate(masks) if i]:
             total = total + other
         held = total
+    return held
+
+
+def gather_pieces(held, stages, parts):
     for masks in reversed(stages):
         got = [send(held, m, parts) for m in masks[1:]]
         held = jnp.concatenate([held] + got, axis=0)
@@ -275,14 +286,18 @@
 
 
 def inverse_root_kernel(
-    me_ref, held_ref, out_ref, packed, full, pval, zhi, zlo, *, masks, side
+    me_ref, held_ref, out_ref, packed, full, pval, zhi, zlo, *, masks, side, blocks, pieces
 ):
     me = me_ref[0]
-    piece = held_ref.shape[1]
-    for t, m in enumerate(masks):
-        packed[pl.ds(pl.multiple_of((me ^ m) * piece, math.gcd(piece, 8)), piece), :] = held_ref[t]
+    start = inner = 0
+    for piece in pieces:
+        for t, m in enumerate(masks):
+            rows = pl.multiple_of(start + (me ^ m) * piece, math.gcd(piece, 8))
+            packed[pl.ds(rows, piece), :] = held_ref[t, inner : inner + piece]
+        start += piece * len(masks)
+        inner += piece
     count = full.shape[0]
-    for at, (i, j) in enumerate(triangle(count, side)):
+    for at, (i, j) in enumerate(blocks):
         tile = packed[at * side : (at + 1) * side, :]
         full[i * side : (i + 1) * side, j * side : (j + 1) * side] = tile
         if i != j:
@@ -318,9 +333,11 @@
     out_ref[...] = (z / jnp.sqrt(scale)).astype(BF)
 
 
-def run_inverse_root(me, held, masks, count, side):
+def run_inverse_root(me, held, masks, count, side, blocks, pieces):
     return pl.pallas_call(
-        functools.partial(inverse_root_kernel, masks=masks, side=side),
+        functools.partial(
+            inverse_root_kernel, masks=masks, side=side, blocks=blocks, pieces=pieces
+        ),
         in_specs=[
             pl.BlockSpec(memory_space=pltpu.SMEM),
             pl.BlockSpec(memory_space=pltpu.VMEM),
@@ -328,7 +345,7 @@
         out_specs=pl.BlockSpec(memory_space=pltpu.VMEM),
         out_shape=jax.ShapeDtypeStruct((count, count), BF),
         scratch_shapes=[
-            pltpu.VMEM((held.shape[0] * held.shape[1], side), F32),
+            pltpu.VMEM((len(blocks) * side, side), F32),
             pltpu.VMEM((count, count), F32),
             pltpu.VMEM((count, count), F32),
             pltpu.VMEM((count, count), BF),
@@ -344,39 +361,38 @@
 
 def rotate_kernel(*refs):
     coeff_ref, ins, out_ref, den_ref, flat = refs[0], refs[1:-3], refs[-3], refs[-2], refs[-1]
-    width = flat.shape[1]
-    start = 0
-    for ref in ins:
-        size = ref.shape[0] * ref.shape[2]
-        flat[start : start + size, :] = ref[:, 0].reshape(size, width)
-        start += size
-    value = jnp.dot(coeff_ref[...], flat[...], preferred_element_type=F32).astype(BF)
-    out_ref[:, 0] = value.reshape(out_ref.shape[0], out_ref.shape[2], width)
-    wide = value.astype(F32)
+    parts, _, sets, group, width = out_ref.shape
+    gather_rows(ins, flat)
+    wide = jnp.dot(coeff_ref[...], flat[...], preferred_element_type=F32)
+    wide = wide.astype(BF).astype(F32)
+    for c in range(sets):
+        own = wide[c * parts * group : (c + 1) * parts * group].reshape(parts, group, width)
+        out_ref[:, 0, c] = own.astype(BF)
     den_ref[...] = jnp.sum(wide * wide, axis=0)[None, None]
 
 
 def run_rotate(coeff, spreads):
     parts, per, group, width = spreads[0].shape
-    count = coeff.shape[1]
+    own, count = coeff.shape
+    sets = own // (parts * group)
     return pl.pallas_call(
         rotate_kernel,
         grid=(per,),
         in_specs=[full_spec(coeff)]
         + [pl.BlockSpec((parts, 1, s.shape[2], width), lambda x: (0, x, 0, 0)) for s in spreads],
         out_specs=[
-            pl.BlockSpec((parts, 1, group, width), lambda x: (0, x, 0, 0)),
+            pl.BlockSpec((parts, 1, sets, group, width), lambda x: (0, x, 0, 0, 0)),
             pl.BlockSpec((1, 1, width), lambda x: (x, 0, 0)),
         ],
         out_shape=[
-            jax.ShapeDtypeStruct((parts, per, group, width), BF),
+            jax.ShapeDtypeStruct((parts, per, sets, group, width), BF),
             jax.ShapeDtypeStruct((per, 1, width), F32),
         ],
         scratch_shapes=[pltpu.VMEM((count, width), BF)],
         compiler_params=pltpu.CompilerParams(vmem_limit_bytes=48 << 20),
         cost_estimate=pl.CostEstimate(
-            flops=2 * count * parts * group * width * per,
-            bytes_accessed=2 * (count + parts * group) * width * per,
+            flops=2 * count * own * width * per,
+            bytes_accessed=2 * (count + own) * width * per,
             transcendentals=0,
         ),
         name="rotate",
@@ -384,30 +400,26 @@
 
 
 def restore_kernel(*refs):
-    in_ref, out_ref, wide = refs[0], refs[-2], refs[-1]
-    parts, per, group, _ = in_ref.shape
-    for s in range(parts):
-        for x in range(per):
-            wide[pl.ds((s * per + x) * group, group), :] = in_ref[s, x].astype(F32)
-    for g in range(group):
-        out_ref[g] = wide[pl.ds(g, parts * per, stride=group), :].astype(BF)
+    in_ref, out_ref = refs[0], refs[-1]
+    parts, per, sets, group, lanes = in_ref.shape
+    wide = in_ref[...].astype(F32).reshape(parts * per, sets * group, lanes)
+    out_ref[...] = jnp.swapaxes(wide, 0, 1).astype(BF)
 
 
 def run_restore(spread, target, chunk, chunks):
-    parts, per, group, width = spread.shape
-    size_x = parts * per
+    parts, per, sets, group, width = spread.shape
+    own, size_x = sets * group, parts * per
     args = (spread,) if target is None else (spread, target)
     return pl.pallas_call(
         restore_kernel,
-        grid=(width // LANES,),
-        in_specs=[pl.BlockSpec((parts, per, group, LANES), lambda l: (0, 0, 0, l))]
+        grid=(width // COLS,),
+        in_specs=[pl.BlockSpec((parts, per, sets, group, COLS), lambda l: (0, 0, 0, 0, l))]
         + [pl.BlockSpec(memory_space=pl.ANY)] * (len(args) - 1),
-        out_specs=pl.BlockSpec((group, size_x, LANES), lambda l: (chunk, 0, l)),
-        out_shape=jax.ShapeDtypeStruct((group * chunks, size_x, width), BF),
-        scratch_shapes=[pltpu.VMEM((size_x * group, LANES), F32)],
+        out_specs=pl.BlockSpec((own, size_x, COLS), lambda l: (chunk, 0, l)),
+        out_shape=jax.ShapeDtypeStruct((own * chunks, size_x, width), BF),
         input_output_aliases={} if target is None else {1: 0},
         cost_estimate=pl.CostEstimate(
-            flops=0, bytes_accessed=4 * group * size_x * width, transcendentals=0
+            flops=0, bytes_accessed=4 * own * size_x * width, transcendentals=0
         ),
         name="restore",
     )(*args)
@@ -416,28 +428,38 @@
 def shards(orbitals, potential):
     parts = lax.axis_size("orb")
     mine, size_x, width = orbitals.shape[1:]
-    group = mine // CHUNKS
+    chunks = max(1, mine // 8)
+    outs = min(chunks, OUT_CHUNKS)
     count = mine * parts
     exchange = lambda v: lax.all_to_all(v, "orb", split_axis=0, concat_axis=0, tiled=True)
-    spreads = []
-    for c in range(CHUNKS):
-        spreads.append(exchange(run_filter(orbitals[0], c, potential, parts, 512)))
     me = lax.axis_index("orb").astype(jnp.int32).reshape(1)
     stages = stage_masks(parts)
     order = piece_order(stages)
-    partial = run_margin(me, spreads, size_x * width, LANES, order)
-    held = reduce_margin(partial, stages, parts)
-    coeff = run_inverse_root(me, held, order, count, LANES)
-    own = group * parts
+    spreads = [
+        exchange(run_filter(orbitals[0], c, chunks, potential, parts, 512))
+        for c in range(chunks)
+    ]
+    early = (chunks - 1) * (count // chunks)
+    blocks = triangle(early, LANES)
+    last = [pair for pair in triangle(count, LANES) if pair not in blocks]
+    helds = []
+    for some, ready in ((blocks, spreads[:-1]), (last, spreads)):
+        if some:
+            partial = run_margin(me, ready, size_x * width, LANES, order, some, helds)
+            helds.append(scatter_sum(partial, stages, parts))
+    held = gather_pieces(jnp.concatenate(helds, axis=1), stages, parts)
+    pieces = [h.shape[1] for h in helds]
+    coeff = run_inverse_root(me, held, order, count, LANES, blocks + last, pieces)
+    own = count // outs
     target = None
     density = 0.0
     returned = []
-    for c in range(CHUNKS):
+    for c in range(outs):
         rotated, part = run_rotate(coeff[c * own : (c + 1) * own], spreads)
         returned.append(exchange(rotated))
         density = density + part[:, 0]
-    for c in range(CHUNKS):
-        target = run_restore(returned[c], target, c, CHUNKS)
+    for c in range(outs):
+        target = run_restore(returned[c], target, c, outs)
     kpoints = lax.axis_size("kpt")
     total = density
     for k in range(1, kpoints):

time: 315 us -> 300 us (0.952)
  waiting for transfers between devices: 156 us -> 120 us
  starting transfers between devices: 38.3 us -> 58.5 us
    all_to_all x4 -> x6, waiting for transfers between devices: 137 us -> 91.7 us  [shards(): lax.all_to_all(v, 'orb', split_axis=0, concat_axis=0, tiled=True)]
    all_to_all x4 -> x6, starting transfers between devices: 22.4 us -> 35.3 us  [shards(): lax.all_to_all(v, 'orb', split_axis=0, concat_axis=0, tiled=True)]
    ppermute x12 -> x18, waiting for transfers between devices: 17.3 us -> 27.2 us  [send(): return lax.ppermute(value, 'orb', [(i, i ^ mask) for i in range(parts)])]
    ppermute x12 -> x18, starting transfers between devices: 15.8 us -> 23.1 us  [send(): return lax.ppermute(value, 'orb', [(i, i ^ mask) for i in range(parts)])]
    pallas_call x2 -> x4, Pallas kernels: 73 us -> 77.4 us  [run_filter(): pl.pallas_call(functools.partial(filter_kernel, first=first, firstt=first...]
    pallas_call x2, Pallas kernels: 12.5 us -> 8.48 us  [run_restore(): pl.pallas_call(restore_kernel, grid=(width // COLS,), in_specs=[pl.BlockS...]
    pallas_call x1 -> x2, Pallas kernels: 5.34 us -> 6.68 us  [run_margin(): pl.pallas_call(functools.partial(margin_kernel, side=side, gain=1.0 / cel...]
  transfers between devices with their start and end apart: 17 -> 25, of which waited for: 14 -> 21; matrix products, arithmetic and copies ran while one was open for 0% -> 0% of each run, Pallas kernels for 15% -> 23%
where the time goes in v1:
time: 300 us; the launch traced here: 299 us
  waiting for transfers between devices  120 us (40%)
  Pallas kernels  118 us (39%)
  starting transfers between devices  58.5 us (20%)
    all_to_all x6, waiting for transfers between devices, shards(): lax.all_to_all(v, 'orb', split_axis=0, concat_axis=0, tiled=True)  91.7 us
    pallas_call x4, Pallas kernels, run_filter(): pl.pallas_call(functools.partial(filter_kernel, first=first, firstt=first...  77.4 us
    all_to_all x6, starting transfers between devices, shards(): lax.all_to_all(v, 'orb', split_axis=0, concat_axis=0, tiled=True)  35.3 us
    ppermute x18, waiting for transfers between devices, send(): return lax.ppermute(value, 'orb', [(i, i ^ mask) for i in range(parts)])  27.2 us
    ppermute x18, starting transfers between devices, send(): return lax.ppermute(value, 'orb', [(i, i ^ mask) for i in range(parts)])  23.1 us
    pallas_call x1, Pallas kernels, run_inverse_root(): pl.pallas_call(functools.partial(inverse_root_kernel, masks=masks, side=s...  16.1 us
    pallas_call x2, Pallas kernels, run_rotate(): pl.pallas_call(rotate_kernel, grid=(per,), in_specs=[full_spec(coeff)] +...  9.13 us
    pallas_call x2, Pallas kernels, run_restore(): pl.pallas_call(restore_kernel, grid=(width // COLS,), in_specs=[pl.BlockS...  8.48 us
  transfers between devices with their start and end apart: 25, of which 21 were waited for; matrix products, arithmetic and copies ran while one was open for 0% of the time, Pallas kernels for 23%

profile of v1, /device:TPU:12, one launch (start us, length us, event | category | flops | bytes accessed | tf_op | source)
XLA Modules:
  0.0 299.4 jit_solution(17826384967389416206)
XLA Ops:
  0.6 19.4 %chebyshev.6 = bf16[16,4,8,1024]{3,2,1,0:T(8,128)(2,1)} custom-call(bf16[32,64,1024]{2,1,0:T(8,128)(2,1)} %bitcast.10, f32[64,1024]{1,0:T(8,128)} %pot_ref.7, bf16[256,256]{1,0:T(8,128)(2,1)} %constant.22.kx_ref, bf16[256,256]{1,0:T(8,128)(2,1)} %constant.23.mx_ref, bf16[1024,256]{1,0:T(8,128)(2,1)} %constant.24.kyz_ref, bf16[768,256]{1,0:T(8,128)(2,1)} %constant.25.myz_ref, ...), custom_call_target="tpu_custom_call" | custom-call | flops 13958643712 | bytes 2097152 | tf_op jit(solution)/shard_map/chebyshev/pallas_call | solution.py:136
  20.0 7.2 %all-to-all-start.2 = ((bf16[16,4,8,1024]{3,2,1,0:T(8,128)(2,1)}), bf16[16,4,8,1024]{3,2,1,0:T(8,128)(2,1)S(1)}, u32[]{:S(2)}, u32[]{:S(2)}) async-start(bf16[16,4,8,1024]{3,2,1,0:T(8,128)(2,1)} %chebyshev.6), calls=%async_computation.2 | async-start | bytes 2097152 | tf_op jit(solution)/shard_map/all_to_all | solution.py:434
  27.2 19.4 %chebyshev.5 = bf16[16,4,8,1024]{3,2,1,0:T(8,128)(2,1)} custom-call(bf16[32,64,1024]{2,1,0:T(8,128)(2,1)} %bitcast.11, f32[64,1024]{1,0:T(8,128)} %pot_ref.7, bf16[256,256]{1,0:T(8,128)(2,1)} %constant.22.kx_ref, bf16[256,256]{1,0:T(8,128)(2,1)} %constant.23.mx_ref, bf16[1024,256]{1,0:T(8,128)(2,1)} %constant.24.kyz_ref, bf16[768,256]{1,0:T(8,128)(2,1)} %constant.25.myz_ref, ...), custom_call_target="tpu_custom_call" | custom-call | flops 13958643712 | bytes 2097152 | tf_op jit(solution)/shard_map/chebyshev/pallas_call | solution.py:136
  46.5 6.0 %all-to-all-done.2.refs_2_.refs_3_ = bf16[16,4,8,1024]{3,2,1,0:T(8,128)(2,1)S(1)} async-done(((bf16[16,4,8,1024]{3,2,1,0:T(8,128)(2,1)}), bf16[16,4,8,1024]{3,2,1,0:T(8,128)(2,1)S(1)}, u32[]{:S(2)}, u32[]{:S(2)}) %all-to-all-start.2) | async-done | bytes 1048608 | tf_op jit(solution)/shard_map/all_to_all | solution.py:434
  52.5 4.9 %all-to-all-start.1 = ((bf16[16,4,8,1024]{3,2,1,0:T(8,128)(2,1)}), bf16[16,4,8,1024]{3,2,1,0:T(8,128)(2,1)S(1)}, u32[]{:S(2)}, u32[]{:S(2)}) async-start(bf16[16,4,8,1024]{3,2,1,0:T(8,128)(2,1)} %chebyshev.5), calls=%async_computation.1 | async-start | bytes 2097152 | tf_op jit(solution)/shard_map/all_to_all | solution.py:434
  57.4 19.4 %chebyshev.4 = bf16[16,4,8,1024]{3,2,1,0:T(8,128)(2,1)} custom-call(bf16[32,64,1024]{2,1,0:T(8,128)(2,1)} %bitcast.12, f32[64,1024]{1,0:T(8,128)} %pot_ref.7, bf16[256,256]{1,0:T(8,128)(2,1)} %constant.22.kx_ref, bf16[256,256]{1,0:T(8,128)(2,1)} %constant.23.mx_ref, bf16[1024,256]{1,0:T(8,128)(2,1)} %constant.24.kyz_ref, bf16[768,256]{1,0:T(8,128)(2,1)} %constant.25.myz_ref, ...), custom_call_target="tpu_custom_call" | custom-call | flops 13958643712 | bytes 2097152 | tf_op jit(solution)/shard_map/chebyshev/pallas_call | solution.py:136
  76.8 4.6 %all-to-all-done.1.refs_1_.refs_2_ = bf16[16,4,8,1024]{3,2,1,0:T(8,128)(2,1)S(1)} async-done(((bf16[16,4,8,1024]{3,2,1,0:T(8,128)(2,1)}), bf16[16,4,8,1024]{3,2,1,0:T(8,128)(2,1)S(1)}, u32[]{:S(2)}, u32[]{:S(2)}) %all-to-all-start.1) | async-done | bytes 1048608 | tf_op jit(solution)/shard_map/all_to_all | solution.py:434
  81.3 5.1 %all-to-all-start = ((bf16[16,4,8,1024]{3,2,1,0:T(8,128)(2,1)}), bf16[16,4,8,1024]{3,2,1,0:T(8,128)(2,1)S(1)}, u32[]{:S(2)}, u32[]{:S(2)}) async-start(bf16[16,4,8,1024]{3,2,1,0:T(8,128)(2,1)} %chebyshev.4), calls=%async_computation | async-start | bytes 2097152 | tf_op jit(solution)/shard_map/all_to_all | solution.py:434
  86.4 19.4 %chebyshev.7 = bf16[16,4,8,1024]{3,2,1,0:T(8,128)(2,1)} custom-call(bf16[32,64,1024]{2,1,0:T(8,128)(2,1)} %bitcast.13, f32[64,1024]{1,0:T(8,128)} %pot_ref.7, bf16[256,256]{1,0:T(8,128)(2,1)} %constant.22.kx_ref, bf16[256,256]{1,0:T(8,128)(2,1)} %constant.23.mx_ref, bf16[1024,256]{1,0:T(8,128)(2,1)} %constant.24.kyz_ref, bf16[768,256]{1,0:T(8,128)(2,1)} %constant.25.myz_ref, ...), custom_call_target="tpu_custom_call" | custom-call | flops 13958643712 | bytes 2097152 | tf_op jit(solution)/shard_map/chebyshev/pallas_call | solution.py:136
  105.8 4.5 %all-to-all-done.refs_0_.refs_1_ = bf16[16,4,8,1024]{3,2,1,0:T(8,128)(2,1)S(1)} async-done(((bf16[16,4,8,1024]{3,2,1,0:T(8,128)(2,1)}), bf16[16,4,8,1024]{3,2,1,0:T(8,128)(2,1)S(1)}, u32[]{:S(2)}, u32[]{:S(2)}) %all-to-all-start) | async-done | bytes 1048608 | tf_op jit(solution)/shard_map/all_to_all | solution.py:434
  110.3 5.1 %all-to-all-start.3 = ((bf16[16,4,8,1024]{3,2,1,0:T(8,128)(2,1)}), bf16[16,4,8,1024]{3,2,1,0:T(8,128)(2,1)}, u32[]{:S(2)}, u32[]{:S(2)}) async-start(bf16[16,4,8,1024]{3,2,1,0:T(8,128)(2,1)} %chebyshev.7), calls=%async_computation.3 | async-start | bytes 2097152 | tf_op jit(solution)/shard_map/all_to_all | solution.py:434
  115.3 3.0 %margin.2 = f32[16,48,128]{2,1,0:T(8,128)S(1)} custom-call(s32[1]{0:T(128)} %bitcast.me_ref, bf16[16,4,8,1024]{3,2,1,0:T(8,128)(2,1)S(1)} %all-to-all-done.refs_0_.refs_1_, bf16[16,4,8,1024]{3,2,1,0:T(8,128)(2,1)S(1)} %all-to-all-done.1.refs_1_.refs_2_, bf16[16,4,8,1024]{3,2,1,0:T(8,128)(2,1)S(1)} %all-to-all-done.2.refs_2_.refs_3_), custom_call_target="tpu_custom_call" | custom-call | flops 805306368 | bytes 3145728 | tf_op jit(solution)/shard_map/margin/pallas_call | solution.py:215
  121.9 2.5 collective-permute-done
  124.4 2.3 collective-permute-done.2
  126.7 1.8 collective-permute-done.1
  130.5 2.5 collective-permute-start.4
  133.0 7.2 %collective-permute-done.5 = f32[1,48,128]{2,1,0:T(8,128)S(1)} collective-permute-done((f32[1,48,128]{2,1,0:T(8,128)S(1)}, f32[1,48,128]{2,1,0:T(8,128)S(1)}, u32[]{:S(2)}, u32[]{:S(2)}) %collective-permute-start.5) | collective-permute-done | bytes 24608 | tf_op jit(solution)/shard_map/ppermute | solution.py:256
  140.9 3.7 %margin.3 = f32[16,32,128]{2,1,0:T(8,128)S(1)} custom-call(s32[1]{0:T(128)} %bitcast.me_ref, bf16[16,4,8,1024]{3,2,1,0:T(8,128)(2,1)S(1)} %all-to-all-done.refs_0_.refs_1_, bf16[16,4,8,1024]{3,2,1,0:T(8,128)(2,1)S(1)} %all-to-all-done.1.refs_1_.refs_2_, bf16[16,4,8,1024]{3,2,1,0:T(8,128)(2,1)S(1)} %all-to-all-done.2.refs_2_.refs_3_, ...), custom_call_target="tpu_custom_call" | custom-call | flops 536870912 | bytes 4194304 | tf_op jit(solution)/shard_map/margin/pallas_call | solution.py:215
  153.2 2.5 collective-permute-start.10
  156.4 1.7 collective-permute-done.10
  158.1 2.9 collective-permute-start.13
  163.1 1.9 collective-permute-done.12
  168.7 4.3 %collective-permute-done.15 = f32[4,80,128]{2,1,0:T(8,128)S(1)} collective-permute-done((f32[4,80,128]{2,1,0:T(8,128)S(1)}, f32[4,80,128]{2,1,0:T(8,128)S(1)}, u32[]{:S(2)}, u32[]{:S(2)}) %collective-permute-start.15) | collective-permute-done | bytes 163872 | tf_op jit(solution)/shard_map/ppermute | solution.py:256
  173.3 16.1 %inverse_root.1 = bf16[512,512]{1,0:T(8,128)(2,1)S(1)} custom-call(s32[1]{0:T(128)} %bitcast.me_ref, f32[16,80,128]{2,1,0:T(8,128)S(1)} %constant_dynamic-update-slice_fusion.held_ref), custom_call_target="tpu_custom_call" | custom-call | flops 13690208256 | bytes 1048576 | tf_op jit(solution)/shard_map/inverse_root/pallas_call | solution.py:337
  189.4 4.5 %rotate.3 = (bf16[16,4,2,8,1024]{4,3,2,1,0:T(8,128)(2,1)}, f32[4,1,1024]{2,1,0:T(1,128)S(1)}) custom-call(bf16[256,512]{1,0:T(8,128)(2,1)S(1)} %get-tuple-element.10.refs_0_, bf16[16,4,8,1024]{3,2,1,0:T(8,128)(2,1)S(1)} %all-to-all-done.refs_0_.refs_1_, bf16[16,4,8,1024]{3,2,1,0:T(8,128)(2,1)S(1)} %all-to-all-done.1.refs_1_.refs_2_, ...), custom_call_target="tpu_custom_call" | custom-call | flops 1073741824 | bytes 6291456 | tf_op jit(solution)/shard_map/rotate/pallas_call | solution.py:378
  194.0 8.2 %all-to-all-start.5 = ((bf16[16,4,2,8,1024]{4,3,2,1,0:T(8,128)(2,1)}), bf16[16,4,2,8,1024]{4,3,2,1,0:T(8,128)(2,1)}, u32[]{:S(2)}, u32[]{:S(2)}) async-start(bf16[16,4,2,8,1024]{4,3,2,1,0:T(8,128)(2,1)} %get-tuple-element.7), calls=%async_computation.5 | async-start | bytes 4194304 | tf_op jit(solution)/shard_map/all_to_all | solution.py:434
  202.2 4.6 %rotate.2 = (bf16[16,4,2,8,1024]{4,3,2,1,0:T(8,128)(2,1)}, f32[4,1,1024]{2,1,0:T(1,128)S(1)}) custom-call(bf16[256,512]{1,0:T(8,128)(2,1)S(1)} %get-tuple-element.11.refs_0_, bf16[16,4,8,1024]{3,2,1,0:T(8,128)(2,1)S(1)} %all-to-all-done.refs_0_.refs_1_, bf16[16,4,8,1024]{3,2,1,0:T(8,128)(2,1)S(1)} %all-to-all-done.1.refs_1_.refs_2_, ...), custom_call_target="tpu_custom_call" | custom-call | flops 1073741824 | bytes 6291456 | tf_op jit(solution)/shard_map/rotate/pallas_call | solution.py:378
  206.8 36.7 %all-to-all-done.5.refs_0_ = bf16[16,4,2,8,1024]{4,3,2,1,0:T(8,128)(2,1)} async-done(((bf16[16,4,2,8,1024]{4,3,2,1,0:T(8,128)(2,1)}), bf16[16,4,2,8,1024]{4,3,2,1,0:T(8,128)(2,1)}, u32[]{:S(2)}, u32[]{:S(2)}) %all-to-all-start.5) | async-done | bytes 2097184 | tf_op jit(solution)/shard_map/all_to_all | solution.py:434
  243.5 4.8 %all-to-all-start.4 = ((bf16[16,4,2,8,1024]{4,3,2,1,0:T(8,128)(2,1)}), bf16[16,4,2,8,1024]{4,3,2,1,0:T(8,128)(2,1)S(1)}, u32[]{:S(2)}, u32[]{:S(2)}) async-start(bf16[16,4,2,8,1024]{4,3,2,1,0:T(8,128)(2,1)} %get-tuple-element.6), calls=%async_computation.4 | async-start | bytes 4194304 | tf_op jit(solution)/shard_map/all_to_all | solution.py:434
  250.1 4.2 %restore.2.refs_1_ = bf16[32,64,1024]{2,1,0:T(8,128)(2,1)} custom-call(bf16[16,4,2,8,1024]{4,3,2,1,0:T(8,128)(2,1)} %all-to-all-done.5.refs_0_), custom_call_target="tpu_custom_call" | custom-call | bytes 4194304 | tf_op jit(solution)/shard_map/restore/pallas_call | solution.py:413
  254.4 39.4 %all-to-all-done.4.refs_0_ = bf16[16,4,2,8,1024]{4,3,2,1,0:T(8,128)(2,1)S(1)} async-done(((bf16[16,4,2,8,1024]{4,3,2,1,0:T(8,128)(2,1)}), bf16[16,4,2,8,1024]{4,3,2,1,0:T(8,128)(2,1)S(1)}, u32[]{:S(2)}, u32[]{:S(2)}) %all-to-all-start.4) | async-done | bytes 2097184 | tf_op jit(solution)/shard_map/all_to_all | solution.py:434
  295.1 4.2 %restore.3 = bf16[32,64,1024]{2,1,0:T(8,128)(2,1)} custom-call(bf16[16,4,2,8,1024]{4,3,2,1,0:T(8,128)(2,1)} %copy-done, bf16[32,64,1024]{2,1,0:T(8,128)(2,1)} %restore.2.refs_1_), custom_call_target="tpu_custom_call", output_to_operand_aliasing={{}: (1, {})} | custom-call | bytes 4194304 | tf_op jit(solution)/shard_map/restore/pallas_call | solution.py:413
  (51 shorter events, 24.7 us)
Async XLA Ops:
  20.0 32.5 %all-to-all-start.2 = ((bf16[16,4,8,1024]{3,2,1,0:T(8,128)(2,1)}), bf16[16,4,8,1024]{3,2,1,0:T(8,128)(2,1)S(1)}, u32[]{:S(2)}, u32[]{:S(2)}) async-start(bf16[16,4,8,1024]{3,2,1,0:T(8,128)(2,1)} %chebyshev.6), calls=%async_computation.2 | async-start | bytes 2097152 | tf_op jit(solution)/shard_map/all_to_all | solution.py:434
  52.5 28.9 %all-to-all-start.1 = ((bf16[16,4,8,1024]{3,2,1,0:T(8,128)(2,1)}), bf16[16,4,8,1024]{3,2,1,0:T(8,128)(2,1)S(1)}, u32[]{:S(2)}, u32[]{:S(2)}) async-start(bf16[16,4,8,1024]{3,2,1,0:T(8,128)(2,1)} %chebyshev.5), calls=%async_computation.1 | async-start | bytes 2097152 | tf_op jit(solution)/shard_map/all_to_all | solution.py:434
  81.3 28.9 %all-to-all-start = ((bf16[16,4,8,1024]{3,2,1,0:T(8,128)(2,1)}), bf16[16,4,8,1024]{3,2,1,0:T(8,128)(2,1)S(1)}, u32[]{:S(2)}, u32[]{:S(2)}) async-start(bf16[16,4,8,1024]{3,2,1,0:T(8,128)(2,1)} %chebyshev.4), calls=%async_computation | async-start | bytes 2097152 | tf_op jit(solution)/shard_map/all_to_all | solution.py:434
  110.3 30.6 %all-to-all-start.3 = ((bf16[16,4,8,1024]{3,2,1,0:T(8,128)(2,1)}), bf16[16,4,8,1024]{3,2,1,0:T(8,128)(2,1)}, u32[]{:S(2)}, u32[]{:S(2)}) async-start(bf16[16,4,8,1024]{3,2,1,0:T(8,128)(2,1)} %chebyshev.7), calls=%async_computation.3 | async-start | bytes 2097152 | tf_op jit(solution)/shard_map/all_to_all | solution.py:434
  118.4 6.0 %collective-permute-start = (f32[4,48,128]{2,1,0:T(8,128)S(1)}, f32[4,48,128]{2,1,0:T(8,128)S(1)}, u32[]{:S(2)}, u32[]{:S(2)}) collective-permute-start(f32[4,48,128]{2,1,0:T(8,128)S(1)} %get-tuple-element.12), channel_id=1, source_target_pairs={{0,1},{1,0},{2,3},{3,2},{4,5},{5,4},{6,7},{7,6},{8,9},{9,8},{10,11... | collective-permute-start | bytes 294920 | tf_op jit(solution)/shard_map/ppermute | solution.py:256
  119.9 6.8 %collective-permute-start.2 = (f32[4,48,128]{2,1,0:T(8,128)S(1)}, f32[4,48,128]{2,1,0:T(8,128)S(1)}, u32[]{:S(2)}, u32[]{:S(2)}) collective-permute-start(f32[4,48,128]{2,1,0:T(8,128)S(1)} %get-tuple-element.13), channel_id=1, source_target_pairs={{0,3},{1,2},{2,1},{3,0},{4,7},{5,6},{6,5},{7,4},{8,11},{9,10},{10,... | collective-permute-start | bytes 294920 | tf_op jit(solution)/shard_map/ppermute | solution.py:256
  120.5 8.0 %collective-permute-start.1 = (f32[4,48,128]{2,1,0:T(8,128)S(1)}, f32[4,48,128]{2,1,0:T(8,128)S(1)}, u32[]{:S(2)}, u32[]{:S(2)}) collective-permute-start(f32[4,48,128]{2,1,0:T(8,128)S(1)} %get-tuple-element.14), channel_id=1, source_target_pairs={{0,2},{1,3},{2,0},{3,1},{4,6},{5,7},{6,4},{7,5},{8,10},{9,11},{10,... | collective-permute-start | bytes 294920 | tf_op jit(solution)/shard_map/ppermute | solution.py:256
  128.6 4.5 %collective-permute-start.3 = (f32[1,48,128]{2,1,0:T(8,128)S(1)}, f32[1,48,128]{2,1,0:T(8,128)S(1)}, u32[]{:S(2)}, u32[]{:S(2)}) collective-permute-start(f32[1,48,128]{2,1,0:T(8,128)S(1)} %get-tuple-element.18), channel_id=1, source_target_pairs={{0,4},{1,5},{2,6},{3,7},{4,0},{5,1},{6,2},{7,3},{8,12},{9,13},{10,... | collective-permute-start | bytes 73736 | tf_op jit(solution)/shard_map/ppermute | solution.py:256
  129.7 10.5 %collective-permute-start.5 = (f32[1,48,128]{2,1,0:T(8,128)S(1)}, f32[1,48,128]{2,1,0:T(8,128)S(1)}, u32[]{:S(2)}, u32[]{:S(2)}) collective-permute-start(f32[1,48,128]{2,1,0:T(8,128)S(1)} %get-tuple-element.19), channel_id=1, source_target_pairs={{0,12},{1,13},{2,14},{3,15},{4,8},{5,9},{6,10},{7,11},{8,4},{9,5},... | collective-permute-start | bytes 73736 | tf_op jit(solution)/shard_map/ppermute | solution.py:256
  130.5 9.7 %collective-permute-start.4 = (f32[1,48,128]{2,1,0:T(8,128)S(1)}, f32[1,48,128]{2,1,0:T(8,128)S(1)}, u32[]{:S(2)}, u32[]{:S(2)}) collective-permute-start(f32[1,48,128]{2,1,0:T(8,128)S(1)} %get-tuple-element.20), channel_id=1, source_target_pairs={{0,8},{1,9},{2,10},{3,11},{4,12},{5,13},{6,14},{7,15},{8,0},{9,1},... | collective-permute-start | bytes 73736 | tf_op jit(solution)/shard_map/ppermute | solution.py:256
  144.6 4.3 %collective-permute-start.6 = (f32[4,32,128]{2,1,0:T(8,128)S(1)}, f32[4,32,128]{2,1,0:T(8,128)S(1)}, u32[]{:S(2)}, u32[]{:S(2)}) collective-permute-start(f32[4,32,128]{2,1,0:T(8,128)S(1)} %get-tuple-element.15), channel_id=1, source_target_pairs={{0,1},{1,0},{2,3},{3,2},{4,5},{5,4},{6,7},{7,6},{8,9},{9,8},{10,11... | collective-permute-start | bytes 196616 | tf_op jit(solution)/shard_map/ppermute | solution.py:256
  145.4 5.2 %collective-permute-start.8 = (f32[4,32,128]{2,1,0:T(8,128)S(1)}, f32[4,32,128]{2,1,0:T(8,128)S(1)}, u32[]{:S(2)}, u32[]{:S(2)}) collective-permute-start(f32[4,32,128]{2,1,0:T(8,128)S(1)} %get-tuple-element.16), channel_id=1, source_target_pairs={{0,3},{1,2},{2,1},{3,0},{4,7},{5,6},{6,5},{7,4},{8,11},{9,10},{10,... | collective-permute-start | bytes 196616 | tf_op jit(solution)/shard_map/ppermute | solution.py:256
  146.6 4.6 %collective-permute-start.7 = (f32[4,32,128]{2,1,0:T(8,128)S(1)}, f32[4,32,128]{2,1,0:T(8,128)S(1)}, u32[]{:S(2)}, u32[]{:S(2)}) collective-permute-start(f32[4,32,128]{2,1,0:T(8,128)S(1)} %get-tuple-element.17), channel_id=1, source_target_pairs={{0,2},{1,3},{2,0},{3,1},{4,6},{5,7},{6,4},{7,5},{8,10},{9,11},{10,... | collective-permute-start | bytes 196616 | tf_op jit(solution)/shard_map/ppermute | solution.py:256
  151.3 4.5 %collective-permute-start.9 = (f32[1,32,128]{2,1,0:T(8,128)S(1)}, f32[1,32,128]{2,1,0:T(8,128)S(1)}, u32[]{:S(2)}, u32[]{:S(2)}) collective-permute-start(f32[1,32,128]{2,1,0:T(8,128)S(1)} %get-tuple-element.21), channel_id=1, source_target_pairs={{0,4},{1,5},{2,6},{3,7},{4,0},{5,1},{6,2},{7,3},{8,12},{9,13},{10,... | collective-permute-start | bytes 49160 | tf_op jit(solution)/shard_map/ppermute | solution.py:256
  152.7 3.7 %collective-permute-start.11 = (f32[1,32,128]{2,1,0:T(8,128)S(1)}, f32[1,32,128]{2,1,0:T(8,128)S(1)}, u32[]{:S(2)}, u32[]{:S(2)}) collective-permute-start(f32[1,32,128]{2,1,0:T(8,128)S(1)} %get-tuple-element.22), channel_id=1, source_target_pairs={{0,12},{1,13},{2,14},{3,15},{4,8},{5,9},{6,10},{7,11},{8,4},{9,5},... | collective-permute-start | bytes 49160 | tf_op jit(solution)/shard_map/ppermute | solution.py:256
  153.2 4.9 %collective-permute-start.10 = (f32[1,32,128]{2,1,0:T(8,128)S(1)}, f32[1,32,128]{2,1,0:T(8,128)S(1)}, u32[]{:S(2)}, u32[]{:S(2)}) collective-permute-start(f32[1,32,128]{2,1,0:T(8,128)S(1)} %get-tuple-element.23), channel_id=1, source_target_pairs={{0,8},{1,9},{2,10},{3,11},{4,12},{5,13},{6,14},{7,15},{8,0},{9,1},... | collective-permute-start | bytes 49160 | tf_op jit(solution)/shard_map/ppermute | solution.py:256
  158.1 5.0 %collective-permute-start.13 = (f32[1,80,128]{2,1,0:T(8,128)S(1)}, f32[1,80,128]{2,1,0:T(8,128)S(1)}, u32[]{:S(2)}, u32[]{:S(2)}) collective-permute-start(f32[1,80,128]{2,1,0:T(8,128)S(1)} %get-tuple-element.24), channel_id=1, source_target_pairs={{0,8},{1,9},{2,10},{3,11},{4,12},{5,13},{6,14},{7,15},{8,0},{9,1},... | collective-permute-start | bytes 122888 | tf_op jit(solution)/shard_map/ppermute | solution.py:256
  161.0 4.0 %collective-permute-start.12 = (f32[1,80,128]{2,1,0:T(8,128)S(1)}, f32[1,80,128]{2,1,0:T(8,128)S(1)}, u32[]{:S(2)}, u32[]{:S(2)}) collective-permute-start(f32[1,80,128]{2,1,0:T(8,128)S(1)} %get-tuple-element.24), channel_id=1, source_target_pairs={{0,4},{1,5},{2,6},{3,7},{4,0},{5,1},{6,2},{7,3},{8,12},{9,13},{10,... | collective-permute-start | bytes 122888 | tf_op jit(solution)/shard_map/ppermute | solution.py:256
  161.2 4.0 %collective-permute-start.14 = (f32[1,80,128]{2,1,0:T(8,128)S(1)}, f32[1,80,128]{2,1,0:T(8,128)S(1)}, u32[]{:S(2)}, u32[]{:S(2)}) collective-permute-start(f32[1,80,128]{2,1,0:T(8,128)S(1)} %get-tuple-element.24), channel_id=1, source_target_pairs={{0,12},{1,13},{2,14},{3,15},{4,8},{5,9},{6,10},{7,11},{8,4},{9,5},... | collective-permute-start | bytes 122888 | tf_op jit(solution)/shard_map/ppermute | solution.py:256
  165.2 8.1 %collective-permute-start.17 = (f32[4,80,128]{2,1,0:T(8,128)S(1)}, f32[4,80,128]{2,1,0:T(8,128)S(1)}, u32[]{:S(2)}, u32[]{:S(2)}) collective-permute-start(f32[4,80,128]{2,1,0:T(8,128)S(1)} %pad_maximum_fusion), channel_id=1, source_target_pairs={{0,3},{1,2},{2,1},{3,0},{4,7},{5,6},{6,5},{7,4},{8,11},{9,10},{10,... | collective-permute-start | bytes 491528 | tf_op jit(solution)/shard_map/ppermute | solution.py:256
  166.7 6.5 %collective-permute-start.16 = (f32[4,80,128]{2,1,0:T(8,128)S(1)}, f32[4,80,128]{2,1,0:T(8,128)S(1)}, u32[]{:S(2)}, u32[]{:S(2)}) collective-permute-start(f32[4,80,128]{2,1,0:T(8,128)S(1)} %pad_maximum_fusion), channel_id=1, source_target_pairs={{0,2},{1,3},{2,0},{3,1},{4,6},{5,7},{6,4},{7,5},{8,10},{9,11},{10,... | collective-permute-start | bytes 491528 | tf_op jit(solution)/shard_map/ppermute | solution.py:256
  167.8 5.3 %collective-permute-start.15 = (f32[4,80,128]{2,1,0:T(8,128)S(1)}, f32[4,80,128]{2,1,0:T(8,128)S(1)}, u32[]{:S(2)}, u32[]{:S(2)}) collective-permute-start(f32[4,80,128]{2,1,0:T(8,128)S(1)} %pad_maximum_fusion), channel_id=1, source_target_pairs={{0,1},{1,0},{2,3},{3,2},{4,5},{5,4},{6,7},{7,6},{8,9},{9,8},{10,11... | collective-permute-start | bytes 491528 | tf_op jit(solution)/shard_map/ppermute | solution.py:256
  194.0 49.5 %all-to-all-start.5 = ((bf16[16,4,2,8,1024]{4,3,2,1,0:T(8,128)(2,1)}), bf16[16,4,2,8,1024]{4,3,2,1,0:T(8,128)(2,1)}, u32[]{:S(2)}, u32[]{:S(2)}) async-start(bf16[16,4,2,8,1024]{4,3,2,1,0:T(8,128)(2,1)} %get-tuple-element.7), calls=%async_computation.5 | async-start | bytes 4194304 | tf_op jit(solution)/shard_map/all_to_all | solution.py:434
  243.5 50.3 %all-to-all-start.4 = ((bf16[16,4,2,8,1024]{4,3,2,1,0:T(8,128)(2,1)}), bf16[16,4,2,8,1024]{4,3,2,1,0:T(8,128)(2,1)S(1)}, u32[]{:S(2)}, u32[]{:S(2)}) async-start(bf16[16,4,2,8,1024]{4,3,2,1,0:T(8,128)(2,1)} %get-tuple-element.6), calls=%async_computation.4 | async-start | bytes 4194304 | tf_op jit(solution)/shard_map/all_to_all | solution.py:434
  248.3 1.2 collective-permute-start.18
  293.8 1.4 copy-start

commit v2 on v1

--- a/solution.py
+++ b/solution.py
@@ -401,23 +401,27 @@
 
 def restore_kernel(*refs):
     in_ref, out_ref = refs[0], refs[-1]
-    parts, per, sets, group, lanes = in_ref.shape
-    wide = in_ref[...].astype(F32).reshape(parts * per, sets * group, lanes)
+    _, per, sets, group, width = in_ref.shape
+    some = out_ref.shape[1] // per
+    first = pl.multiple_of(pl.program_id(0) * some, some)
+    wide = in_ref[pl.ds(first, some)].astype(F32).reshape(some * per, sets * group, width)
     out_ref[...] = jnp.swapaxes(wide, 0, 1).astype(BF)
 
 
 def run_restore(spread, target, chunk, chunks):
     parts, per, sets, group, width = spread.shape
     own, size_x = sets * group, parts * per
+    rows = max(16, per)
     args = (spread,) if target is None else (spread, target)
     return pl.pallas_call(
         restore_kernel,
-        grid=(width // COLS,),
-        in_specs=[pl.BlockSpec((parts, per, sets, group, COLS), lambda l: (0, 0, 0, 0, l))]
+        grid=(size_x // rows,),
+        in_specs=[pl.BlockSpec(memory_space=pltpu.VMEM)]
         + [pl.BlockSpec(memory_space=pl.ANY)] * (len(args) - 1),
-        out_specs=pl.BlockSpec((own, size_x, COLS), lambda l: (chunk, 0, l)),
+        out_specs=pl.BlockSpec((own, rows, width), lambda x: (chunk, x, 0)),
         out_shape=jax.ShapeDtypeStruct((own * chunks, size_x, width), BF),
         input_output_aliases={} if target is None else {1: 0},
+        compiler_params=pltpu.CompilerParams(vmem_limit_bytes=48 << 20),
         cost_estimate=pl.CostEstimate(
             flops=0, bytes_accessed=4 * own * size_x * width, transcendentals=0
         ),
@@ -446,8 +450,9 @@
     for some, ready in ((blocks, spreads[:-1]), (last, spreads)):
         if some:
             partial = run_margin(me, ready, size_x * width, LANES, order, some, helds)
-            helds.append(scatter_sum(partial, stages, parts))
-    held = gather_pieces(jnp.concatenate(helds, axis=1), stages, parts)
+            helds.append(scatter_sum(partial, stages[:1], parts))
+    held = scatter_sum(jnp.concatenate(helds, axis=1), stages[1:], parts)
+    held = gather_pieces(held, stages, parts)
     pieces = [h.shape[1] for h in helds]
     coeff = run_inverse_root(me, held, order, count, LANES, blocks + last, pieces)
     own = count // outs

time: 300 us -> 296 us (0.987)
  starting transfers between devices: 58.5 us -> 52.1 us
  waiting for transfers between devices: 120 us -> 126 us
    all_to_all x6, waiting for transfers between devices: 91.7 us -> 104 us  [shards(): lax.all_to_all(v, 'orb', split_axis=0, concat_axis=0, tiled=True)]
    ppermute x18 -> x15, waiting for transfers between devices: 27.2 us -> 20.6 us  [send(): return lax.ppermute(value, 'orb', [(i, i ^ mask) for i in range(parts)])]
    ppermute x18 -> x15, starting transfers between devices: 23.1 us -> 19.6 us  [send(): return lax.ppermute(value, 'orb', [(i, i ^ mask) for i in range(parts)])]
  transfers between devices with their start and end apart: 25 -> 22, of which waited for: 21 -> 18; matrix products, arithmetic and copies ran while one was open for 0% -> 0% of each run, Pallas kernels for 23% -> 24%
where the time goes in v2:
time: 296 us; the launch traced here: 295 us
  waiting for transfers between devices  126 us (43%)
  Pallas kernels  116 us (39%)
  starting transfers between devices  52.1 us (18%)
    all_to_all x6, waiting for transfers between devices, shards(): lax.all_to_all(v, 'orb', split_axis=0, concat_axis=0, tiled=True)  104 us
    pallas_call x4, Pallas kernels, run_filter(): pl.pallas_call(functools.partial(filter_kernel, first=first, firstt=first...  77.5 us
    all_to_all x6, starting transfers between devices, shards(): lax.all_to_all(v, 'orb', split_axis=0, concat_axis=0, tiled=True)  32.5 us
    ppermute x15, waiting for transfers between devices, send(): return lax.ppermute(value, 'orb', [(i, i ^ mask) for i in range(parts)])  20.6 us
    ppermute x15, starting transfers between devices, send(): return lax.ppermute(value, 'orb', [(i, i ^ mask) for i in range(parts)])  19.6 us
    pallas_call x1, Pallas kernels, run_inverse_root(): pl.pallas_call(functools.partial(inverse_root_kernel, masks=masks, side=s...  16.1 us
    pallas_call x2, Pallas kernels, run_rotate(): pl.pallas_call(rotate_kernel, grid=(per,), in_specs=[full_spec(coeff)] +...  9.13 us
    pallas_call x2, Pallas kernels, run_margin(): pl.pallas_call(functools.partial(margin_kernel, side=side, gain=1.0 / cel...  6.67 us
  transfers between devices with their start and end apart: 22, of which 18 were waited for; matrix products, arithmetic and copies ran while one was open for 0% of the time, Pallas kernels for 24%

profile of v2, /device:TPU:12, one launch (start us, length us, event | category | flops | bytes accessed | tf_op | source)
XLA Modules:
  0.0 295.3 jit_solution(5355093843643358261)
XLA Ops:
  0.6 19.4 %chebyshev.6 = bf16[16,4,8,1024]{3,2,1,0:T(8,128)(2,1)} custom-call(bf16[32,64,1024]{2,1,0:T(8,128)(2,1)} %bitcast.10, f32[64,1024]{1,0:T(8,128)} %pot_ref.7, bf16[256,256]{1,0:T(8,128)(2,1)} %constant.22.kx_ref, bf16[256,256]{1,0:T(8,128)(2,1)} %constant.23.mx_ref, bf16[1024,256]{1,0:T(8,128)(2,1)} %constant.24.kyz_ref, bf16[768,256]{1,0:T(8,128)(2,1)} %constant.25.myz_ref, ...), custom_call_target="tpu_custom_call" | custom-call | flops 13958643712 | bytes 2097152 | tf_op jit(solution)/shard_map/chebyshev/pallas_call | solution.py:136
  20.0 7.2 %all-to-all-start.2 = ((bf16[16,4,8,1024]{3,2,1,0:T(8,128)(2,1)}), bf16[16,4,8,1024]{3,2,1,0:T(8,128)(2,1)S(1)}, u32[]{:S(2)}, u32[]{:S(2)}) async-start(bf16[16,4,8,1024]{3,2,1,0:T(8,128)(2,1)} %chebyshev.6), calls=%async_computation.2 | async-start | bytes 2097152 | tf_op jit(solution)/shard_map/all_to_all | solution.py:438
  27.2 19.4 %chebyshev.5 = bf16[16,4,8,1024]{3,2,1,0:T(8,128)(2,1)} custom-call(bf16[32,64,1024]{2,1,0:T(8,128)(2,1)} %bitcast.11, f32[64,1024]{1,0:T(8,128)} %pot_ref.7, bf16[256,256]{1,0:T(8,128)(2,1)} %constant.22.kx_ref, bf16[256,256]{1,0:T(8,128)(2,1)} %constant.23.mx_ref, bf16[1024,256]{1,0:T(8,128)(2,1)} %constant.24.kyz_ref, bf16[768,256]{1,0:T(8,128)(2,1)} %constant.25.myz_ref, ...), custom_call_target="tpu_custom_call" | custom-call | flops 13958643712 | bytes 2097152 | tf_op jit(solution)/shard_map/chebyshev/pallas_call | solution.py:136
  46.5 6.0 %all-to-all-done.2.refs_2_.refs_3_ = bf16[16,4,8,1024]{3,2,1,0:T(8,128)(2,1)S(1)} async-done(((bf16[16,4,8,1024]{3,2,1,0:T(8,128)(2,1)}), bf16[16,4,8,1024]{3,2,1,0:T(8,128)(2,1)S(1)}, u32[]{:S(2)}, u32[]{:S(2)}) %all-to-all-start.2) | async-done | bytes 1048608 | tf_op jit(solution)/shard_map/all_to_all | solution.py:438
  52.5 4.9 %all-to-all-start.1 = ((bf16[16,4,8,1024]{3,2,1,0:T(8,128)(2,1)}), bf16[16,4,8,1024]{3,2,1,0:T(8,128)(2,1)S(1)}, u32[]{:S(2)}, u32[]{:S(2)}) async-start(bf16[16,4,8,1024]{3,2,1,0:T(8,128)(2,1)} %chebyshev.5), calls=%async_computation.1 | async-start | bytes 2097152 | tf_op jit(solution)/shard_map/all_to_all | solution.py:438
  57.4 19.4 %chebyshev.4 = bf16[16,4,8,1024]{3,2,1,0:T(8,128)(2,1)} custom-call(bf16[32,64,1024]{2,1,0:T(8,128)(2,1)} %bitcast.12, f32[64,1024]{1,0:T(8,128)} %pot_ref.7, bf16[256,256]{1,0:T(8,128)(2,1)} %constant.22.kx_ref, bf16[256,256]{1,0:T(8,128)(2,1)} %constant.23.mx_ref, bf16[1024,256]{1,0:T(8,128)(2,1)} %constant.24.kyz_ref, bf16[768,256]{1,0:T(8,128)(2,1)} %constant.25.myz_ref, ...), custom_call_target="tpu_custom_call" | custom-call | flops 13958643712 | bytes 2097152 | tf_op jit(solution)/shard_map/chebyshev/pallas_call | solution.py:136
  76.8 4.6 %all-to-all-done.1.refs_1_.refs_2_ = bf16[16,4,8,1024]{3,2,1,0:T(8,128)(2,1)S(1)} async-done(((bf16[16,4,8,1024]{3,2,1,0:T(8,128)(2,1)}), bf16[16,4,8,1024]{3,2,1,0:T(8,128)(2,1)S(1)}, u32[]{:S(2)}, u32[]{:S(2)}) %all-to-all-start.1) | async-done | bytes 1048608 | tf_op jit(solution)/shard_map/all_to_all | solution.py:438
  81.3 5.1 %all-to-all-start = ((bf16[16,4,8,1024]{3,2,1,0:T(8,128)(2,1)}), bf16[16,4,8,1024]{3,2,1,0:T(8,128)(2,1)S(1)}, u32[]{:S(2)}, u32[]{:S(2)}) async-start(bf16[16,4,8,1024]{3,2,1,0:T(8,128)(2,1)} %chebyshev.4), calls=%async_computation | async-start | bytes 2097152 | tf_op jit(solution)/shard_map/all_to_all | solution.py:438
  86.4 19.4 %chebyshev.7 = bf16[16,4,8,1024]{3,2,1,0:T(8,128)(2,1)} custom-call(bf16[32,64,1024]{2,1,0:T(8,128)(2,1)} %bitcast.13, f32[64,1024]{1,0:T(8,128)} %pot_ref.7, bf16[256,256]{1,0:T(8,128)(2,1)} %constant.22.kx_ref, bf16[256,256]{1,0:T(8,128)(2,1)} %constant.23.mx_ref, bf16[1024,256]{1,0:T(8,128)(2,1)} %constant.24.kyz_ref, bf16[768,256]{1,0:T(8,128)(2,1)} %constant.25.myz_ref, ...), custom_call_target="tpu_custom_call" | custom-call | flops 13958643712 | bytes 2097152 | tf_op jit(solution)/shard_map/chebyshev/pallas_call | solution.py:136
  105.8 4.5 %all-to-all-done.refs_0_.refs_1_ = bf16[16,4,8,1024]{3,2,1,0:T(8,128)(2,1)S(1)} async-done(((bf16[16,4,8,1024]{3,2,1,0:T(8,128)(2,1)}), bf16[16,4,8,1024]{3,2,1,0:T(8,128)(2,1)S(1)}, u32[]{:S(2)}, u32[]{:S(2)}) %all-to-all-start) | async-done | bytes 1048608 | tf_op jit(solution)/shard_map/all_to_all | solution.py:438
  110.3 5.1 %all-to-all-start.3 = ((bf16[16,4,8,1024]{3,2,1,0:T(8,128)(2,1)}), bf16[16,4,8,1024]{3,2,1,0:T(8,128)(2,1)}, u32[]{:S(2)}, u32[]{:S(2)}) async-start(bf16[16,4,8,1024]{3,2,1,0:T(8,128)(2,1)} %chebyshev.7), calls=%async_computation.3 | async-start | bytes 2097152 | tf_op jit(solution)/shard_map/all_to_all | solution.py:438
  115.3 3.0 %margin.2 = f32[16,48,128]{2,1,0:T(8,128)S(1)} custom-call(s32[1]{0:T(128)} %bitcast.me_ref, bf16[16,4,8,1024]{3,2,1,0:T(8,128)(2,1)S(1)} %all-to-all-done.refs_0_.refs_1_, bf16[16,4,8,1024]{3,2,1,0:T(8,128)(2,1)S(1)} %all-to-all-done.1.refs_1_.refs_2_, bf16[16,4,8,1024]{3,2,1,0:T(8,128)(2,1)S(1)} %all-to-all-done.2.refs_2_.refs_3_), custom_call_target="tpu_custom_call" | custom-call | flops 805306368 | bytes 3145728 | tf_op jit(solution)/shard_map/margin/pallas_call | solution.py:215
  121.9 2.5 collective-permute-done
  124.4 2.3 collective-permute-done.2
  126.7 1.8 collective-permute-done.1
  128.5 10.8 %all-to-all-done.3.refs_3_.refs_4_ = bf16[16,4,8,1024]{3,2,1,0:T(8,128)(2,1)} async-done(((bf16[16,4,8,1024]{3,2,1,0:T(8,128)(2,1)}), bf16[16,4,8,1024]{3,2,1,0:T(8,128)(2,1)}, u32[]{:S(2)}, u32[]{:S(2)}) %all-to-all-start.3) | async-done | bytes 1048608 | tf_op jit(solution)/shard_map/all_to_all | solution.py:438
  139.3 3.7 %margin.3 = f32[16,32,128]{2,1,0:T(8,128)S(1)} custom-call(s32[1]{0:T(128)} %bitcast.me_ref, bf16[16,4,8,1024]{3,2,1,0:T(8,128)(2,1)S(1)} %all-to-all-done.refs_0_.refs_1_, bf16[16,4,8,1024]{3,2,1,0:T(8,128)(2,1)S(1)} %all-to-all-done.1.refs_1_.refs_2_, bf16[16,4,8,1024]{3,2,1,0:T(8,128)(2,1)S(1)} %all-to-all-done.2.refs_2_.refs_3_, ...), custom_call_target="tpu_custom_call" | custom-call | flops 536870912 | bytes 4194304 | tf_op jit(solution)/shard_map/margin/pallas_call | solution.py:215
  149.7 1.8 collective-permute-start.8
  151.5 2.6 collective-permute-start.7
  154.1 2.5 collective-permute-done.7
  157.2 3.8 %collective-permute-start.10 = (f32[1,80,128]{2,1,0:T(8,128)S(1)}, f32[1,80,128]{2,1,0:T(8,128)S(1)}, u32[]{:S(2)}, u32[]{:S(2)}) collective-permute-start(f32[1,80,128]{2,1,0:T(8,128)S(1)} %get-tuple-element.11), channel_id=1, source_target_pairs={{0,8},{1,9},{2,10},{3,11},{4,12},{5,13},{6,14},{7,15},{8,0},{9,1},... | collective-permute-start | bytes 122888 | tf_op jit(solution)/shard_map/ppermute | solution.py:256
  161.1 2.4 collective-permute-done.10
  168.7 4.4 %collective-permute-done.12 = f32[4,80,128]{2,1,0:T(8,128)S(1)} collective-permute-done((f32[4,80,128]{2,1,0:T(8,128)S(1)}, f32[4,80,128]{2,1,0:T(8,128)S(1)}, u32[]{:S(2)}, u32[]{:S(2)}) %collective-permute-start.12) | collective-permute-done | bytes 163872 | tf_op jit(solution)/shard_map/ppermute | solution.py:256
  173.2 16.1 %inverse_root.1 = bf16[512,512]{1,0:T(8,128)(2,1)S(1)} custom-call(s32[1]{0:T(128)} %bitcast.me_ref, f32[16,80,128]{2,1,0:T(8,128)S(1)} %constant_dynamic-update-slice_fusion.held_ref), custom_call_target="tpu_custom_call" | custom-call | flops 13690208256 | bytes 1048576 | tf_op jit(solution)/shard_map/inverse_root/pallas_call | solution.py:337
  189.4 4.5 %rotate.3 = (bf16[16,4,2,8,1024]{4,3,2,1,0:T(8,128)(2,1)}, f32[4,1,1024]{2,1,0:T(1,128)S(1)}) custom-call(bf16[256,512]{1,0:T(8,128)(2,1)S(1)} %get-tuple-element.12.refs_0_, bf16[16,4,8,1024]{3,2,1,0:T(8,128)(2,1)S(1)} %all-to-all-done.refs_0_.refs_1_, bf16[16,4,8,1024]{3,2,1,0:T(8,128)(2,1)S(1)} %all-to-all-done.1.refs_1_.refs_2_, ...), custom_call_target="tpu_custom_call" | custom-call | flops 1073741824 | bytes 6291456 | tf_op jit(solution)/shard_map/rotate/pallas_call | solution.py:378
  193.9 5.4 %all-to-all-start.5 = ((bf16[16,4,2,8,1024]{4,3,2,1,0:T(8,128)(2,1)}), bf16[16,4,2,8,1024]{4,3,2,1,0:T(8,128)(2,1)}, u32[]{:S(2)}, u32[]{:S(2)}) async-start(bf16[16,4,2,8,1024]{4,3,2,1,0:T(8,128)(2,1)} %get-tuple-element.7), calls=%async_computation.5 | async-start | bytes 4194304 | tf_op jit(solution)/shard_map/all_to_all | solution.py:438
  199.3 4.6 %rotate.2 = (bf16[16,4,2,8,1024]{4,3,2,1,0:T(8,128)(2,1)}, f32[4,1,1024]{2,1,0:T(1,128)S(1)}) custom-call(bf16[256,512]{1,0:T(8,128)(2,1)S(1)} %get-tuple-element.13.refs_0_, bf16[16,4,8,1024]{3,2,1,0:T(8,128)(2,1)S(1)} %all-to-all-done.refs_0_.refs_1_, bf16[16,4,8,1024]{3,2,1,0:T(8,128)(2,1)S(1)} %all-to-all-done.1.refs_1_.refs_2_, ...), custom_call_target="tpu_custom_call" | custom-call | flops 1073741824 | bytes 6291456 | tf_op jit(solution)/shard_map/rotate/pallas_call | solution.py:378
  203.9 37.6 %all-to-all-done.5.refs_0_ = bf16[16,4,2,8,1024]{4,3,2,1,0:T(8,128)(2,1)} async-done(((bf16[16,4,2,8,1024]{4,3,2,1,0:T(8,128)(2,1)}), bf16[16,4,2,8,1024]{4,3,2,1,0:T(8,128)(2,1)}, u32[]{:S(2)}, u32[]{:S(2)}) %all-to-all-start.5) | async-done | bytes 2097184 | tf_op jit(solution)/shard_map/all_to_all | solution.py:438
  241.5 4.9 %all-to-all-start.4 = ((bf16[16,4,2,8,1024]{4,3,2,1,0:T(8,128)(2,1)}), bf16[16,4,2,8,1024]{4,3,2,1,0:T(8,128)(2,1)S(1)}, u32[]{:S(2)}, u32[]{:S(2)}) async-start(bf16[16,4,2,8,1024]{4,3,2,1,0:T(8,128)(2,1)} %get-tuple-element.6), calls=%async_computation.4 | async-start | bytes 4194304 | tf_op jit(solution)/shard_map/all_to_all | solution.py:438
  248.2 4.0 %restore.2.refs_1_ = bf16[32,64,1024]{2,1,0:T(8,128)(2,1)} custom-call(bf16[16,4,2,8,1024]{4,3,2,1,0:T(8,128)(2,1)} %all-to-all-done.5.refs_0_), custom_call_target="tpu_custom_call" | custom-call | bytes 4194304 | tf_op jit(solution)/shard_map/restore/pallas_call | solution.py:416
  252.2 40.7 %all-to-all-done.4.refs_0_ = bf16[16,4,2,8,1024]{4,3,2,1,0:T(8,128)(2,1)S(1)} async-done(((bf16[16,4,2,8,1024]{4,3,2,1,0:T(8,128)(2,1)}), bf16[16,4,2,8,1024]{4,3,2,1,0:T(8,128)(2,1)S(1)}, u32[]{:S(2)}, u32[]{:S(2)}) %all-to-all-start.4) | async-done | bytes 2097184 | tf_op jit(solution)/shard_map/all_to_all | solution.py:438
  292.9 2.4 restore.3
  (40 shorter events, 18.2 us)
Async XLA Ops:
  20.0 32.5 %all-to-all-start.2 = ((bf16[16,4,8,1024]{3,2,1,0:T(8,128)(2,1)}), bf16[16,4,8,1024]{3,2,1,0:T(8,128)(2,1)S(1)}, u32[]{:S(2)}, u32[]{:S(2)}) async-start(bf16[16,4,8,1024]{3,2,1,0:T(8,128)(2,1)} %chebyshev.6), calls=%async_computation.2 | async-start | bytes 2097152 | tf_op jit(solution)/shard_map/all_to_all | solution.py:438
  52.5 28.9 %all-to-all-start.1 = ((bf16[16,4,8,1024]{3,2,1,0:T(8,128)(2,1)}), bf16[16,4,8,1024]{3,2,1,0:T(8,128)(2,1)S(1)}, u32[]{:S(2)}, u32[]{:S(2)}) async-start(bf16[16,4,8,1024]{3,2,1,0:T(8,128)(2,1)} %chebyshev.5), calls=%async_computation.1 | async-start | bytes 2097152 | tf_op jit(solution)/shard_map/all_to_all | solution.py:438
  81.3 28.9 %all-to-all-start = ((bf16[16,4,8,1024]{3,2,1,0:T(8,128)(2,1)}), bf16[16,4,8,1024]{3,2,1,0:T(8,128)(2,1)S(1)}, u32[]{:S(2)}, u32[]{:S(2)}) async-start(bf16[16,4,8,1024]{3,2,1,0:T(8,128)(2,1)} %chebyshev.4), calls=%async_computation | async-start | bytes 2097152 | tf_op jit(solution)/shard_map/all_to_all | solution.py:438
  110.3 29.0 %all-to-all-start.3 = ((bf16[16,4,8,1024]{3,2,1,0:T(8,128)(2,1)}), bf16[16,4,8,1024]{3,2,1,0:T(8,128)(2,1)}, u32[]{:S(2)}, u32[]{:S(2)}) async-start(bf16[16,4,8,1024]{3,2,1,0:T(8,128)(2,1)} %chebyshev.7), calls=%async_computation.3 | async-start | bytes 2097152 | tf_op jit(solution)/shard_map/all_to_all | solution.py:438
  118.4 6.0 %collective-permute-start = (f32[4,48,128]{2,1,0:T(8,128)S(1)}, f32[4,48,128]{2,1,0:T(8,128)S(1)}, u32[]{:S(2)}, u32[]{:S(2)}) collective-permute-start(f32[4,48,128]{2,1,0:T(8,128)S(1)} %get-tuple-element.14), channel_id=1, source_target_pairs={{0,1},{1,0},{2,3},{3,2},{4,5},{5,4},{6,7},{7,6},{8,9},{9,8},{10,11... | collective-permute-start | bytes 294920 | tf_op jit(solution)/shard_map/ppermute | solution.py:256
  119.9 6.8 %collective-permute-start.2 = (f32[4,48,128]{2,1,0:T(8,128)S(1)}, f32[4,48,128]{2,1,0:T(8,128)S(1)}, u32[]{:S(2)}, u32[]{:S(2)}) collective-permute-start(f32[4,48,128]{2,1,0:T(8,128)S(1)} %get-tuple-element.15), channel_id=1, source_target_pairs={{0,3},{1,2},{2,1},{3,0},{4,7},{5,6},{6,5},{7,4},{8,11},{9,10},{10,... | collective-permute-start | bytes 294920 | tf_op jit(solution)/shard_map/ppermute | solution.py:256
  120.5 8.0 %collective-permute-start.1 = (f32[4,48,128]{2,1,0:T(8,128)S(1)}, f32[4,48,128]{2,1,0:T(8,128)S(1)}, u32[]{:S(2)}, u32[]{:S(2)}) collective-permute-start(f32[4,48,128]{2,1,0:T(8,128)S(1)} %get-tuple-element.16), channel_id=1, source_target_pairs={{0,2},{1,3},{2,0},{3,1},{4,6},{5,7},{6,4},{7,5},{8,10},{9,11},{10,... | collective-permute-start | bytes 294920 | tf_op jit(solution)/shard_map/ppermute | solution.py:256
  143.0 4.3 %collective-permute-start.3 = (f32[4,32,128]{2,1,0:T(8,128)S(1)}, f32[4,32,128]{2,1,0:T(8,128)S(1)}, u32[]{:S(2)}, u32[]{:S(2)}) collective-permute-start(f32[4,32,128]{2,1,0:T(8,128)S(1)} %get-tuple-element.17), channel_id=1, source_target_pairs={{0,1},{1,0},{2,3},{3,2},{4,5},{5,4},{6,7},{7,6},{8,9},{9,8},{10,11... | collective-permute-start | bytes 196616 | tf_op jit(solution)/shard_map/ppermute | solution.py:256
  143.7 5.2 %collective-permute-start.5 = (f32[4,32,128]{2,1,0:T(8,128)S(1)}, f32[4,32,128]{2,1,0:T(8,128)S(1)}, u32[]{:S(2)}, u32[]{:S(2)}) collective-permute-start(f32[4,32,128]{2,1,0:T(8,128)S(1)} %get-tuple-element.18), channel_id=1, source_target_pairs={{0,3},{1,2},{2,1},{3,0},{4,7},{5,6},{6,5},{7,4},{8,11},{9,10},{10,... | collective-permute-start | bytes 196616 | tf_op jit(solution)/shard_map/ppermute | solution.py:256
  145.3 4.3 %collective-permute-start.4 = (f32[4,32,128]{2,1,0:T(8,128)S(1)}, f32[4,32,128]{2,1,0:T(8,128)S(1)}, u32[]{:S(2)}, u32[]{:S(2)}) collective-permute-start(f32[4,32,128]{2,1,0:T(8,128)S(1)} %get-tuple-element.19), channel_id=1, source_target_pairs={{0,2},{1,3},{2,0},{3,1},{4,6},{5,7},{6,4},{7,5},{8,10},{9,11},{10,... | collective-permute-start | bytes 196616 | tf_op jit(solution)/shard_map/ppermute | solution.py:256
  149.6 4.5 %collective-permute-start.6 = (f32[1,80,128]{2,1,0:T(8,128)S(1)}, f32[1,80,128]{2,1,0:T(8,128)S(1)}, u32[]{:S(2)}, u32[]{:S(2)}) collective-permute-start(f32[1,80,128]{2,1,0:T(8,128)S(1)} %get-tuple-element.20), channel_id=1, source_target_pairs={{0,4},{1,5},{2,6},{3,7},{4,0},{5,1},{6,2},{7,3},{8,12},{9,13},{10,... | collective-permute-start | bytes 122888 | tf_op jit(solution)/shard_map/ppermute | solution.py:256
  149.7 4.4 %collective-permute-start.8 = (f32[1,80,128]{2,1,0:T(8,128)S(1)}, f32[1,80,128]{2,1,0:T(8,128)S(1)}, u32[]{:S(2)}, u32[]{:S(2)}) collective-permute-start(f32[1,80,128]{2,1,0:T(8,128)S(1)} %get-tuple-element.21), channel_id=1, source_target_pairs={{0,12},{1,13},{2,14},{3,15},{4,8},{5,9},{6,10},{7,11},{8,4},{9,5},... | collective-permute-start | bytes 122888 | tf_op jit(solution)/shard_map/ppermute | solution.py:256
  151.5 5.1 %collective-permute-start.7 = (f32[1,80,128]{2,1,0:T(8,128)S(1)}, f32[1,80,128]{2,1,0:T(8,128)S(1)}, u32[]{:S(2)}, u32[]{:S(2)}) collective-permute-start(f32[1,80,128]{2,1,0:T(8,128)S(1)} %get-tuple-element.22), channel_id=1, source_target_pairs={{0,8},{1,9},{2,10},{3,11},{4,12},{5,13},{6,14},{7,15},{8,0},{9,1},... | collective-permute-start | bytes 122888 | tf_op jit(solution)/shard_map/ppermute | solution.py:256
  156.6 4.5 %collective-permute-start.11 = (f32[1,80,128]{2,1,0:T(8,128)S(1)}, f32[1,80,128]{2,1,0:T(8,128)S(1)}, u32[]{:S(2)}, u32[]{:S(2)}) collective-permute-start(f32[1,80,128]{2,1,0:T(8,128)S(1)} %get-tuple-element.11), channel_id=1, source_target_pairs={{0,12},{1,13},{2,14},{3,15},{4,8},{5,9},{6,10},{7,11},{8,4},{9,5},... | collective-permute-start | bytes 122888 | tf_op jit(solution)/shard_map/ppermute | solution.py:256
  157.2 6.2 %collective-permute-start.10 = (f32[1,80,128]{2,1,0:T(8,128)S(1)}, f32[1,80,128]{2,1,0:T(8,128)S(1)}, u32[]{:S(2)}, u32[]{:S(2)}) collective-permute-start(f32[1,80,128]{2,1,0:T(8,128)S(1)} %get-tuple-element.11), channel_id=1, source_target_pairs={{0,8},{1,9},{2,10},{3,11},{4,12},{5,13},{6,14},{7,15},{8,0},{9,1},... | collective-permute-start | bytes 122888 | tf_op jit(solution)/shard_map/ppermute | solution.py:256
  161.1 4.0 %collective-permute-start.9 = (f32[1,80,128]{2,1,0:T(8,128)S(1)}, f32[1,80,128]{2,1,0:T(8,128)S(1)}, u32[]{:S(2)}, u32[]{:S(2)}) collective-permute-start(f32[1,80,128]{2,1,0:T(8,128)S(1)} %get-tuple-element.11), channel_id=1, source_target_pairs={{0,4},{1,5},{2,6},{3,7},{4,0},{5,1},{6,2},{7,3},{8,12},{9,13},{10,... | collective-permute-start | bytes 122888 | tf_op jit(solution)/shard_map/ppermute | solution.py:256
  165.1 8.1 %collective-permute-start.14 = (f32[4,80,128]{2,1,0:T(8,128)S(1)}, f32[4,80,128]{2,1,0:T(8,128)S(1)}, u32[]{:S(2)}, u32[]{:S(2)}) collective-permute-start(f32[4,80,128]{2,1,0:T(8,128)S(1)} %pad_maximum_fusion), channel_id=1, source_target_pairs={{0,3},{1,2},{2,1},{3,0},{4,7},{5,6},{6,5},{7,4},{8,11},{9,10},{10,... | collective-permute-start | bytes 491528 | tf_op jit(solution)/shard_map/ppermute | solution.py:256
  166.5 6.6 %collective-permute-start.13 = (f32[4,80,128]{2,1,0:T(8,128)S(1)}, f32[4,80,128]{2,1,0:T(8,128)S(1)}, u32[]{:S(2)}, u32[]{:S(2)}) collective-permute-start(f32[4,80,128]{2,1,0:T(8,128)S(1)} %pad_maximum_fusion), channel_id=1, source_target_pairs={{0,2},{1,3},{2,0},{3,1},{4,6},{5,7},{6,4},{7,5},{8,10},{9,11},{10,... | collective-permute-start | bytes 491528 | tf_op jit(solution)/shard_map/ppermute | solution.py:256
  167.7 5.3 %collective-permute-start.12 = (f32[4,80,128]{2,1,0:T(8,128)S(1)}, f32[4,80,128]{2,1,0:T(8,128)S(1)}, u32[]{:S(2)}, u32[]{:S(2)}) collective-permute-start(f32[4,80,128]{2,1,0:T(8,128)S(1)} %pad_maximum_fusion), channel_id=1, source_target_pairs={{0,1},{1,0},{2,3},{3,2},{4,5},{5,4},{6,7},{7,6},{8,9},{9,8},{10,11... | collective-permute-start | bytes 491528 | tf_op jit(solution)/shard_map/ppermute | solution.py:256
  193.9 47.6 %all-to-all-start.5 = ((bf16[16,4,2,8,1024]{4,3,2,1,0:T(8,128)(2,1)}), bf16[16,4,2,8,1024]{4,3,2,1,0:T(8,128)(2,1)}, u32[]{:S(2)}, u32[]{:S(2)}) async-start(bf16[16,4,2,8,1024]{4,3,2,1,0:T(8,128)(2,1)} %get-tuple-element.7), calls=%async_computation.5 | async-start | bytes 4194304 | tf_op jit(solution)/shard_map/all_to_all | solution.py:438
  241.5 51.4 %all-to-all-start.4 = ((bf16[16,4,2,8,1024]{4,3,2,1,0:T(8,128)(2,1)}), bf16[16,4,2,8,1024]{4,3,2,1,0:T(8,128)(2,1)S(1)}, u32[]{:S(2)}, u32[]{:S(2)}) async-start(bf16[16,4,2,8,1024]{4,3,2,1,0:T(8,128)(2,1)} %get-tuple-element.6), calls=%async_computation.4 | async-start | bytes 4194304 | tf_op jit(solution)/shard_map/all_to_all | solution.py:438
  246.4 1.2 collective-permute-start.15

commit v3 on v2

--- a/solution.py
+++ b/solution.py
@@ -13,7 +13,7 @@
 ITERS = 8
 LANES = 128
 COLS = 256
-OUT_CHUNKS = 2
+OUT_CHUNKS = 1
 BF = jnp.bfloat16
 F32 = jnp.float32
 

time: 296 us -> 294 us (level)
  waiting for transfers between devices: 126 us -> 132 us
  starting transfers between devices: 52.1 us -> 47.3 us
  Pallas kernels: 116 us -> 112 us
    all_to_all x6 -> x5, waiting for transfers between devices: 104 us -> 111 us  [shards(): lax.all_to_all(v, 'orb', split_axis=0, concat_axis=0, tiled=True)]
    all_to_all x6 -> x5, starting transfers between devices: 32.5 us -> 27.6 us  [shards(): lax.all_to_all(v, 'orb', split_axis=0, concat_axis=0, tiled=True)]
    pallas_call x2 -> x1, Pallas kernels: 9.13 us -> 5.64 us  [run_rotate(): pl.pallas_call(rotate_kernel, grid=(per,), in_specs=[full_spec(coeff)] +...]
    pallas_call x2 -> x1, Pallas kernels: 6.4 us -> 5.74 us  [run_restore(): pl.pallas_call(restore_kernel, grid=(size_x // rows,), in_specs=[pl.Block...]
  transfers between devices with their start and end apart: 22 -> 21, of which waited for: 18 -> 17; matrix products, arithmetic and copies ran while one was open for 0% -> 0% of each run, Pallas kernels for 24% -> 21%
where the time goes in v3:
time: 294 us; the launch traced here: 293 us
  waiting for transfers between devices  132 us (45%)
  Pallas kernels  112 us (38%)
  starting transfers between devices  47.3 us (16%)
    all_to_all x5, waiting for transfers between devices, shards(): lax.all_to_all(v, 'orb', split_axis=0, concat_axis=0, tiled=True)  111 us
    pallas_call x4, Pallas kernels, run_filter(): pl.pallas_call(functools.partial(filter_kernel, first=first, firstt=first...  77.4 us
    all_to_all x5, starting transfers between devices, shards(): lax.all_to_all(v, 'orb', split_axis=0, concat_axis=0, tiled=True)  27.6 us
    ppermute x15, waiting for transfers between devices, send(): return lax.ppermute(value, 'orb', [(i, i ^ mask) for i in range(parts)])  20.5 us
    ppermute x15, starting transfers between devices, send(): return lax.ppermute(value, 'orb', [(i, i ^ mask) for i in range(parts)])  19.6 us
    pallas_call x1, Pallas kernels, run_inverse_root(): pl.pallas_call(functools.partial(inverse_root_kernel, masks=masks, side=s...  16.1 us
    pallas_call x2, Pallas kernels, run_margin(): pl.pallas_call(functools.partial(margin_kernel, side=side, gain=1.0 / cel...  6.67 us
  transfers between devices with their start and end apart: 21, of which 17 were waited for; matrix products, arithmetic and copies ran while one was open for 0% of the time, Pallas kernels for 21%

profile of v3, /device:TPU:12, one launch (start us, length us, event | category | flops | bytes accessed | tf_op | source)
XLA Modules:
  0.0 292.9 jit_solution(5119866050992225251)
XLA Ops:
  0.6 19.4 %chebyshev.6 = bf16[16,4,8,1024]{3,2,1,0:T(8,128)(2,1)} custom-call(bf16[32,64,1024]{2,1,0:T(8,128)(2,1)} %bitcast.10, f32[64,1024]{1,0:T(8,128)} %pot_ref.7, bf16[256,256]{1,0:T(8,128)(2,1)} %constant.22.kx_ref, bf16[256,256]{1,0:T(8,128)(2,1)} %constant.23.mx_ref, bf16[1024,256]{1,0:T(8,128)(2,1)} %constant.24.kyz_ref, bf16[768,256]{1,0:T(8,128)(2,1)} %constant.25.myz_ref, ...), custom_call_target="tpu_custom_call" | custom-call | flops 13958643712 | bytes 2097152 | tf_op jit(solution)/shard_map/chebyshev/pallas_call | solution.py:136
  20.0 7.2 %all-to-all-start.2 = ((bf16[16,4,8,1024]{3,2,1,0:T(8,128)(2,1)}), bf16[16,4,8,1024]{3,2,1,0:T(8,128)(2,1)S(1)}, u32[]{:S(2)}, u32[]{:S(2)}) async-start(bf16[16,4,8,1024]{3,2,1,0:T(8,128)(2,1)} %chebyshev.6), calls=%async_computation.2 | async-start | bytes 2097152 | tf_op jit(solution)/shard_map/all_to_all | solution.py:438
  27.2 19.4 %chebyshev.5 = bf16[16,4,8,1024]{3,2,1,0:T(8,128)(2,1)} custom-call(bf16[32,64,1024]{2,1,0:T(8,128)(2,1)} %bitcast.11, f32[64,1024]{1,0:T(8,128)} %pot_ref.7, bf16[256,256]{1,0:T(8,128)(2,1)} %constant.22.kx_ref, bf16[256,256]{1,0:T(8,128)(2,1)} %constant.23.mx_ref, bf16[1024,256]{1,0:T(8,128)(2,1)} %constant.24.kyz_ref, bf16[768,256]{1,0:T(8,128)(2,1)} %constant.25.myz_ref, ...), custom_call_target="tpu_custom_call" | custom-call | flops 13958643712 | bytes 2097152 | tf_op jit(solution)/shard_map/chebyshev/pallas_call | solution.py:136
  46.5 6.0 %all-to-all-done.2.refs_2_.refs_3_ = bf16[16,4,8,1024]{3,2,1,0:T(8,128)(2,1)S(1)} async-done(((bf16[16,4,8,1024]{3,2,1,0:T(8,128)(2,1)}), bf16[16,4,8,1024]{3,2,1,0:T(8,128)(2,1)S(1)}, u32[]{:S(2)}, u32[]{:S(2)}) %all-to-all-start.2) | async-done | bytes 1048608 | tf_op jit(solution)/shard_map/all_to_all | solution.py:438
  52.5 4.9 %all-to-all-start.1 = ((bf16[16,4,8,1024]{3,2,1,0:T(8,128)(2,1)}), bf16[16,4,8,1024]{3,2,1,0:T(8,128)(2,1)S(1)}, u32[]{:S(2)}, u32[]{:S(2)}) async-start(bf16[16,4,8,1024]{3,2,1,0:T(8,128)(2,1)} %chebyshev.5), calls=%async_computation.1 | async-start | bytes 2097152 | tf_op jit(solution)/shard_map/all_to_all | solution.py:438
  57.4 19.4 %chebyshev.4 = bf16[16,4,8,1024]{3,2,1,0:T(8,128)(2,1)} custom-call(bf16[32,64,1024]{2,1,0:T(8,128)(2,1)} %bitcast.12, f32[64,1024]{1,0:T(8,128)} %pot_ref.7, bf16[256,256]{1,0:T(8,128)(2,1)} %constant.22.kx_ref, bf16[256,256]{1,0:T(8,128)(2,1)} %constant.23.mx_ref, bf16[1024,256]{1,0:T(8,128)(2,1)} %constant.24.kyz_ref, bf16[768,256]{1,0:T(8,128)(2,1)} %constant.25.myz_ref, ...), custom_call_target="tpu_custom_call" | custom-call | flops 13958643712 | bytes 2097152 | tf_op jit(solution)/shard_map/chebyshev/pallas_call | solution.py:136
  76.8 4.6 %all-to-all-done.1.refs_1_.refs_2_ = bf16[16,4,8,1024]{3,2,1,0:T(8,128)(2,1)S(1)} async-done(((bf16[16,4,8,1024]{3,2,1,0:T(8,128)(2,1)}), bf16[16,4,8,1024]{3,2,1,0:T(8,128)(2,1)S(1)}, u32[]{:S(2)}, u32[]{:S(2)}) %all-to-all-start.1) | async-done | bytes 1048608 | tf_op jit(solution)/shard_map/all_to_all | solution.py:438
  81.3 5.1 %all-to-all-start = ((bf16[16,4,8,1024]{3,2,1,0:T(8,128)(2,1)}), bf16[16,4,8,1024]{3,2,1,0:T(8,128)(2,1)S(1)}, u32[]{:S(2)}, u32[]{:S(2)}) async-start(bf16[16,4,8,1024]{3,2,1,0:T(8,128)(2,1)} %chebyshev.4), calls=%async_computation | async-start | bytes 2097152 | tf_op jit(solution)/shard_map/all_to_all | solution.py:438
  86.4 19.4 %chebyshev.7 = bf16[16,4,8,1024]{3,2,1,0:T(8,128)(2,1)} custom-call(bf16[32,64,1024]{2,1,0:T(8,128)(2,1)} %bitcast.13, f32[64,1024]{1,0:T(8,128)} %pot_ref.7, bf16[256,256]{1,0:T(8,128)(2,1)} %constant.22.kx_ref, bf16[256,256]{1,0:T(8,128)(2,1)} %constant.23.mx_ref, bf16[1024,256]{1,0:T(8,128)(2,1)} %constant.24.kyz_ref, bf16[768,256]{1,0:T(8,128)(2,1)} %constant.25.myz_ref, ...), custom_call_target="tpu_custom_call" | custom-call | flops 13958643712 | bytes 2097152 | tf_op jit(solution)/shard_map/chebyshev/pallas_call | solution.py:136
  105.8 4.5 %all-to-all-done.refs_0_.refs_1_ = bf16[16,4,8,1024]{3,2,1,0:T(8,128)(2,1)S(1)} async-done(((bf16[16,4,8,1024]{3,2,1,0:T(8,128)(2,1)}), bf16[16,4,8,1024]{3,2,1,0:T(8,128)(2,1)S(1)}, u32[]{:S(2)}, u32[]{:S(2)}) %all-to-all-start) | async-done | bytes 1048608 | tf_op jit(solution)/shard_map/all_to_all | solution.py:438
  110.3 5.1 %all-to-all-start.3 = ((bf16[16,4,8,1024]{3,2,1,0:T(8,128)(2,1)}), bf16[16,4,8,1024]{3,2,1,0:T(8,128)(2,1)}, u32[]{:S(2)}, u32[]{:S(2)}) async-start(bf16[16,4,8,1024]{3,2,1,0:T(8,128)(2,1)} %chebyshev.7), calls=%async_computation.3 | async-start | bytes 2097152 | tf_op jit(solution)/shard_map/all_to_all | solution.py:438
  115.3 3.0 %margin.2 = f32[16,48,128]{2,1,0:T(8,128)S(1)} custom-call(s32[1]{0:T(128)} %bitcast.me_ref, bf16[16,4,8,1024]{3,2,1,0:T(8,128)(2,1)S(1)} %all-to-all-done.refs_0_.refs_1_, bf16[16,4,8,1024]{3,2,1,0:T(8,128)(2,1)S(1)} %all-to-all-done.1.refs_1_.refs_2_, bf16[16,4,8,1024]{3,2,1,0:T(8,128)(2,1)S(1)} %all-to-all-done.2.refs_2_.refs_3_), custom_call_target="tpu_custom_call" | custom-call | flops 805306368 | bytes 3145728 | tf_op jit(solution)/shard_map/margin/pallas_call | solution.py:215
  118.4 1.5 collective-permute-start
  121.9 2.5 collective-permute-done
  124.4 2.3 collective-permute-done.2
  126.7 1.8 collective-permute-done.1
  128.5 10.8 %all-to-all-done.3.refs_3_.refs_4_ = bf16[16,4,8,1024]{3,2,1,0:T(8,128)(2,1)} async-done(((bf16[16,4,8,1024]{3,2,1,0:T(8,128)(2,1)}), bf16[16,4,8,1024]{3,2,1,0:T(8,128)(2,1)}, u32[]{:S(2)}, u32[]{:S(2)}) %all-to-all-start.3) | async-done | bytes 1048608 | tf_op jit(solution)/shard_map/all_to_all | solution.py:438
  139.3 3.7 %margin.3 = f32[16,32,128]{2,1,0:T(8,128)S(1)} custom-call(s32[1]{0:T(128)} %bitcast.me_ref, bf16[16,4,8,1024]{3,2,1,0:T(8,128)(2,1)S(1)} %all-to-all-done.refs_0_.refs_1_, bf16[16,4,8,1024]{3,2,1,0:T(8,128)(2,1)S(1)} %all-to-all-done.1.refs_1_.refs_2_, bf16[16,4,8,1024]{3,2,1,0:T(8,128)(2,1)S(1)} %all-to-all-done.2.refs_2_.refs_3_, ...), custom_call_target="tpu_custom_call" | custom-call | flops 536870912 | bytes 4194304 | tf_op jit(solution)/shard_map/margin/pallas_call | solution.py:215
  143.7 1.6 collective-permute-start.5
  147.3 1.5 collective-permute-done.5
  149.7 1.8 collective-permute-start.8
  151.5 2.6 collective-permute-start.7
  154.1 2.5 collective-permute-done.7
  157.2 3.9 %collective-permute-start.10 = (f32[1,80,128]{2,1,0:T(8,128)S(1)}, f32[1,80,128]{2,1,0:T(8,128)S(1)}, u32[]{:S(2)}, u32[]{:S(2)}) collective-permute-start(f32[1,80,128]{2,1,0:T(8,128)S(1)} %get-tuple-element.7), channel_id=1, source_target_pairs={{0,8},{1,9},{2,10},{3,11},{4,12},{5,13},{6,14},{7,15},{8,0},{9,1},... | collective-permute-start | bytes 122888 | tf_op jit(solution)/shard_map/ppermute | solution.py:256
  161.1 2.4 collective-permute-done.10
  163.5 1.6 collective-permute-done.9
  168.7 4.3 %collective-permute-done.12 = f32[4,80,128]{2,1,0:T(8,128)S(1)} collective-permute-done((f32[4,80,128]{2,1,0:T(8,128)S(1)}, f32[4,80,128]{2,1,0:T(8,128)S(1)}, u32[]{:S(2)}, u32[]{:S(2)}) %collective-permute-start.12) | collective-permute-done | bytes 163872 | tf_op jit(solution)/shard_map/ppermute | solution.py:256
  173.2 16.1 %inverse_root.1.refs_0_ = bf16[512,512]{1,0:T(8,128)(2,1)S(1)} custom-call(s32[1]{0:T(128)} %bitcast.me_ref, f32[16,80,128]{2,1,0:T(8,128)S(1)} %constant_dynamic-update-slice_fusion.held_ref), custom_call_target="tpu_custom_call" | custom-call | flops 13690208256 | bytes 1048576 | tf_op jit(solution)/shard_map/inverse_root/pallas_call | solution.py:337
  189.3 5.6 %rotate.1 = (bf16[16,4,4,8,1024]{4,3,2,1,0:T(8,128)(2,1)}, f32[4,1,1024]{2,1,0:T(1,128)S(1)}) custom-call(bf16[512,512]{1,0:T(8,128)(2,1)S(1)} %inverse_root.1.refs_0_, bf16[16,4,8,1024]{3,2,1,0:T(8,128)(2,1)S(1)} %all-to-all-done.refs_0_.refs_1_, bf16[16,4,8,1024]{3,2,1,0:T(8,128)(2,1)S(1)} %all-to-all-done.1.refs_1_.refs_2_, ...), custom_call_target="tpu_custom_call" | custom-call | flops 2147483648 | bytes 8388608 | tf_op jit(solution)/shard_map/rotate/pallas_call | solution.py:378
  195.0 5.3 %all-to-all-start.4 = ((bf16[16,4,4,8,1024]{4,3,2,1,0:T(8,128)(2,1)}), bf16[16,4,4,8,1024]{4,3,2,1,0:T(8,128)(2,1)}, u32[]{:S(2)}, u32[]{:S(2)}) async-start(bf16[16,4,4,8,1024]{4,3,2,1,0:T(8,128)(2,1)} %get-tuple-element.4), calls=%async_computation.4 | async-start | bytes 8388608 | tf_op jit(solution)/shard_map/all_to_all | solution.py:438
  202.2 85.0 %all-to-all-done.4.refs_0_ = bf16[16,4,4,8,1024]{4,3,2,1,0:T(8,128)(2,1)} async-done(((bf16[16,4,4,8,1024]{4,3,2,1,0:T(8,128)(2,1)}), bf16[16,4,4,8,1024]{4,3,2,1,0:T(8,128)(2,1)}, u32[]{:S(2)}, u32[]{:S(2)}) %all-to-all-start.4) | async-done | bytes 4194336 | tf_op jit(solution)/shard_map/all_to_all | solution.py:438
  287.2 5.7 %restore.1 = bf16[32,64,1024]{2,1,0:T(8,128)(2,1)} custom-call(bf16[16,4,4,8,1024]{4,3,2,1,0:T(8,128)(2,1)} %all-to-all-done.4.refs_0_), custom_call_target="tpu_custom_call" | custom-call | bytes 8388608 | tf_op jit(solution)/shard_map/restore/pallas_call | solution.py:416
  (34 shorter events, 11.8 us)
Async XLA Ops:
  20.0 32.5 %all-to-all-start.2 = ((bf16[16,4,8,1024]{3,2,1,0:T(8,128)(2,1)}), bf16[16,4,8,1024]{3,2,1,0:T(8,128)(2,1)S(1)}, u32[]{:S(2)}, u32[]{:S(2)}) async-start(bf16[16,4,8,1024]{3,2,1,0:T(8,128)(2,1)} %chebyshev.6), calls=%async_computation.2 | async-start | bytes 2097152 | tf_op jit(solution)/shard_map/all_to_all | solution.py:438
  52.5 28.9 %all-to-all-start.1 = ((bf16[16,4,8,1024]{3,2,1,0:T(8,128)(2,1)}), bf16[16,4,8,1024]{3,2,1,0:T(8,128)(2,1)S(1)}, u32[]{:S(2)}, u32[]{:S(2)}) async-start(bf16[16,4,8,1024]{3,2,1,0:T(8,128)(2,1)} %chebyshev.5), calls=%async_computation.1 | async-start | bytes 2097152 | tf_op jit(solution)/shard_map/all_to_all | solution.py:438
  81.3 28.9 %all-to-all-start = ((bf16[16,4,8,1024]{3,2,1,0:T(8,128)(2,1)}), bf16[16,4,8,1024]{3,2,1,0:T(8,128)(2,1)S(1)}, u32[]{:S(2)}, u32[]{:S(2)}) async-start(bf16[16,4,8,1024]{3,2,1,0:T(8,128)(2,1)} %chebyshev.4), calls=%async_computation | async-start | bytes 2097152 | tf_op jit(solution)/shard_map/all_to_all | solution.py:438
  110.3 29.0 %all-to-all-start.3 = ((bf16[16,4,8,1024]{3,2,1,0:T(8,128)(2,1)}), bf16[16,4,8,1024]{3,2,1,0:T(8,128)(2,1)}, u32[]{:S(2)}, u32[]{:S(2)}) async-start(bf16[16,4,8,1024]{3,2,1,0:T(8,128)(2,1)} %chebyshev.7), calls=%async_computation.3 | async-start | bytes 2097152 | tf_op jit(solution)/shard_map/all_to_all | solution.py:438
  118.4 6.0 %collective-permute-start = (f32[4,48,128]{2,1,0:T(8,128)S(1)}, f32[4,48,128]{2,1,0:T(8,128)S(1)}, u32[]{:S(2)}, u32[]{:S(2)}) collective-permute-start(f32[4,48,128]{2,1,0:T(8,128)S(1)} %get-tuple-element.8), channel_id=1, source_target_pairs={{0,1},{1,0},{2,3},{3,2},{4,5},{5,4},{6,7},{7,6},{8,9},{9,8},{10,11... | collective-permute-start | bytes 294920 | tf_op jit(solution)/shard_map/ppermute | solution.py:256
  119.9 6.8 %collective-permute-start.2 = (f32[4,48,128]{2,1,0:T(8,128)S(1)}, f32[4,48,128]{2,1,0:T(8,128)S(1)}, u32[]{:S(2)}, u32[]{:S(2)}) collective-permute-start(f32[4,48,128]{2,1,0:T(8,128)S(1)} %get-tuple-element.9), channel_id=1, source_target_pairs={{0,3},{1,2},{2,1},{3,0},{4,7},{5,6},{6,5},{7,4},{8,11},{9,10},{10,... | collective-permute-start | bytes 294920 | tf_op jit(solution)/shard_map/ppermute | solution.py:256
  120.5 8.0 %collective-permute-start.1 = (f32[4,48,128]{2,1,0:T(8,128)S(1)}, f32[4,48,128]{2,1,0:T(8,128)S(1)}, u32[]{:S(2)}, u32[]{:S(2)}) collective-permute-start(f32[4,48,128]{2,1,0:T(8,128)S(1)} %get-tuple-element.10), channel_id=1, source_target_pairs={{0,2},{1,3},{2,0},{3,1},{4,6},{5,7},{6,4},{7,5},{8,10},{9,11},{10,... | collective-permute-start | bytes 294920 | tf_op jit(solution)/shard_map/ppermute | solution.py:256
  143.0 4.3 %collective-permute-start.3 = (f32[4,32,128]{2,1,0:T(8,128)S(1)}, f32[4,32,128]{2,1,0:T(8,128)S(1)}, u32[]{:S(2)}, u32[]{:S(2)}) collective-permute-start(f32[4,32,128]{2,1,0:T(8,128)S(1)} %get-tuple-element.11), channel_id=1, source_target_pairs={{0,1},{1,0},{2,3},{3,2},{4,5},{5,4},{6,7},{7,6},{8,9},{9,8},{10,11... | collective-permute-start | bytes 196616 | tf_op jit(solution)/shard_map/ppermute | solution.py:256
  143.7 5.2 %collective-permute-start.5 = (f32[4,32,128]{2,1,0:T(8,128)S(1)}, f32[4,32,128]{2,1,0:T(8,128)S(1)}, u32[]{:S(2)}, u32[]{:S(2)}) collective-permute-start(f32[4,32,128]{2,1,0:T(8,128)S(1)} %get-tuple-element.12), channel_id=1, source_target_pairs={{0,3},{1,2},{2,1},{3,0},{4,7},{5,6},{6,5},{7,4},{8,11},{9,10},{10,... | collective-permute-start | bytes 196616 | tf_op jit(solution)/shard_map/ppermute | solution.py:256
  145.3 4.3 %collective-permute-start.4 = (f32[4,32,128]{2,1,0:T(8,128)S(1)}, f32[4,32,128]{2,1,0:T(8,128)S(1)}, u32[]{:S(2)}, u32[]{:S(2)}) collective-permute-start(f32[4,32,128]{2,1,0:T(8,128)S(1)} %get-tuple-element.13), channel_id=1, source_target_pairs={{0,2},{1,3},{2,0},{3,1},{4,6},{5,7},{6,4},{7,5},{8,10},{9,11},{10,... | collective-permute-start | bytes 196616 | tf_op jit(solution)/shard_map/ppermute | solution.py:256
  149.6 4.5 %collective-permute-start.6 = (f32[1,80,128]{2,1,0:T(8,128)S(1)}, f32[1,80,128]{2,1,0:T(8,128)S(1)}, u32[]{:S(2)}, u32[]{:S(2)}) collective-permute-start(f32[1,80,128]{2,1,0:T(8,128)S(1)} %get-tuple-element.14), channel_id=1, source_target_pairs={{0,4},{1,5},{2,6},{3,7},{4,0},{5,1},{6,2},{7,3},{8,12},{9,13},{10,... | collective-permute-start | bytes 122888 | tf_op jit(solution)/shard_map/ppermute | solution.py:256
  149.7 4.4 %collective-permute-start.8 = (f32[1,80,128]{2,1,0:T(8,128)S(1)}, f32[1,80,128]{2,1,0:T(8,128)S(1)}, u32[]{:S(2)}, u32[]{:S(2)}) collective-permute-start(f32[1,80,128]{2,1,0:T(8,128)S(1)} %get-tuple-element.15), channel_id=1, source_target_pairs={{0,12},{1,13},{2,14},{3,15},{4,8},{5,9},{6,10},{7,11},{8,4},{9,5},... | collective-permute-start | bytes 122888 | tf_op jit(solution)/shard_map/ppermute | solution.py:256
  151.5 5.1 %collective-permute-start.7 = (f32[1,80,128]{2,1,0:T(8,128)S(1)}, f32[1,80,128]{2,1,0:T(8,128)S(1)}, u32[]{:S(2)}, u32[]{:S(2)}) collective-permute-start(f32[1,80,128]{2,1,0:T(8,128)S(1)} %get-tuple-element.16), channel_id=1, source_target_pairs={{0,8},{1,9},{2,10},{3,11},{4,12},{5,13},{6,14},{7,15},{8,0},{9,1},... | collective-permute-start | bytes 122888 | tf_op jit(solution)/shard_map/ppermute | solution.py:256
  156.6 4.5 %collective-permute-start.11 = (f32[1,80,128]{2,1,0:T(8,128)S(1)}, f32[1,80,128]{2,1,0:T(8,128)S(1)}, u32[]{:S(2)}, u32[]{:S(2)}) collective-permute-start(f32[1,80,128]{2,1,0:T(8,128)S(1)} %get-tuple-element.7), channel_id=1, source_target_pairs={{0,12},{1,13},{2,14},{3,15},{4,8},{5,9},{6,10},{7,11},{8,4},{9,5},... | collective-permute-start | bytes 122888 | tf_op jit(solution)/shard_map/ppermute | solution.py:256
  157.2 6.3 %collective-permute-start.10 = (f32[1,80,128]{2,1,0:T(8,128)S(1)}, f32[1,80,128]{2,1,0:T(8,128)S(1)}, u32[]{:S(2)}, u32[]{:S(2)}) collective-permute-start(f32[1,80,128]{2,1,0:T(8,128)S(1)} %get-tuple-element.7), channel_id=1, source_target_pairs={{0,8},{1,9},{2,10},{3,11},{4,12},{5,13},{6,14},{7,15},{8,0},{9,1},... | collective-permute-start | bytes 122888 | tf_op jit(solution)/shard_map/ppermute | solution.py:256
  161.1 4.0 %collective-permute-start.9 = (f32[1,80,128]{2,1,0:T(8,128)S(1)}, f32[1,80,128]{2,1,0:T(8,128)S(1)}, u32[]{:S(2)}, u32[]{:S(2)}) collective-permute-start(f32[1,80,128]{2,1,0:T(8,128)S(1)} %get-tuple-element.7), channel_id=1, source_target_pairs={{0,4},{1,5},{2,6},{3,7},{4,0},{5,1},{6,2},{7,3},{8,12},{9,13},{10,... | collective-permute-start | bytes 122888 | tf_op jit(solution)/shard_map/ppermute | solution.py:256
  165.1 8.1 %collective-permute-start.14 = (f32[4,80,128]{2,1,0:T(8,128)S(1)}, f32[4,80,128]{2,1,0:T(8,128)S(1)}, u32[]{:S(2)}, u32[]{:S(2)}) collective-permute-start(f32[4,80,128]{2,1,0:T(8,128)S(1)} %pad_maximum_fusion), channel_id=1, source_target_pairs={{0,3},{1,2},{2,1},{3,0},{4,7},{5,6},{6,5},{7,4},{8,11},{9,10},{10,... | collective-permute-start | bytes 491528 | tf_op jit(solution)/shard_map/ppermute | solution.py:256
  166.5 6.6 %collective-permute-start.13 = (f32[4,80,128]{2,1,0:T(8,128)S(1)}, f32[4,80,128]{2,1,0:T(8,128)S(1)}, u32[]{:S(2)}, u32[]{:S(2)}) collective-permute-start(f32[4,80,128]{2,1,0:T(8,128)S(1)} %pad_maximum_fusion), channel_id=1, source_target_pairs={{0,2},{1,3},{2,0},{3,1},{4,6},{5,7},{6,4},{7,5},{8,10},{9,11},{10,... | collective-permute-start | bytes 491528 | tf_op jit(solution)/shard_map/ppermute | solution.py:256
  167.7 5.3 %collective-permute-start.12 = (f32[4,80,128]{2,1,0:T(8,128)S(1)}, f32[4,80,128]{2,1,0:T(8,128)S(1)}, u32[]{:S(2)}, u32[]{:S(2)}) collective-permute-start(f32[4,80,128]{2,1,0:T(8,128)S(1)} %pad_maximum_fusion), channel_id=1, source_target_pairs={{0,1},{1,0},{2,3},{3,2},{4,5},{5,4},{6,7},{7,6},{8,9},{9,8},{10,11... | collective-permute-start | bytes 491528 | tf_op jit(solution)/shard_map/ppermute | solution.py:256
  195.0 92.2 %all-to-all-start.4 = ((bf16[16,4,4,8,1024]{4,3,2,1,0:T(8,128)(2,1)}), bf16[16,4,4,8,1024]{4,3,2,1,0:T(8,128)(2,1)}, u32[]{:S(2)}, u32[]{:S(2)}) async-start(bf16[16,4,4,8,1024]{4,3,2,1,0:T(8,128)(2,1)} %get-tuple-element.4), calls=%async_computation.4 | async-start | bytes 8388608 | tf_op jit(solution)/shard_map/all_to_all | solution.py:438
  200.3 1.2 collective-permute-start.15

commit v4 on v3

--- a/solution.py
+++ b/solution.py
@@ -401,10 +401,9 @@
 
 def restore_kernel(*refs):
     in_ref, out_ref = refs[0], refs[-1]
-    _, per, sets, group, width = in_ref.shape
-    some = out_ref.shape[1] // per
-    first = pl.multiple_of(pl.program_id(0) * some, some)
-    wide = in_ref[pl.ds(first, some)].astype(F32).reshape(some * per, sets * group, width)
+    _, _, sets, group, width = in_ref.shape
+    rows = out_ref.shape[1]
+    wide = in_ref[...].astype(F32).reshape(rows, sets * group, width)
     out_ref[...] = jnp.swapaxes(wide, 0, 1).astype(BF)
 
 
@@ -416,7 +415,9 @@
     return pl.pallas_call(
         restore_kernel,
         grid=(size_x // rows,),
-        in_specs=[pl.BlockSpec(memory_space=pltpu.VMEM)]
+        in_specs=[
+            pl.BlockSpec((rows // per, per, sets, group, width), lambda x: (x, 0, 0, 0, 0))
+        ]
         + [pl.BlockSpec(memory_space=pl.ANY)] * (len(args) - 1),
         out_specs=pl.BlockSpec((own, rows, width), lambda x: (chunk, x, 0)),
         out_shape=jax.ShapeDtypeStruct((own * chunks, size_x, width), BF),

time: 294 us -> 294 us (level)
  no operation moved by 1% of the time
where the time goes in v4:
time: 294 us; the launch traced here: 293 us
  waiting for transfers between devices  132 us (45%)
  Pallas kernels  112 us (38%)
  starting transfers between devices  47.3 us (16%)
    all_to_all x5, waiting for transfers between devices, shards(): lax.all_to_all(v, 'orb', split_axis=0, concat_axis=0, tiled=True)  111 us
    pallas_call x4, Pallas kernels, run_filter(): pl.pallas_call(functools.partial(filter_kernel, first=first, firstt=first...  77.4 us
    all_to_all x5, starting transfers between devices, shards(): lax.all_to_all(v, 'orb', split_axis=0, concat_axis=0, tiled=True)  27.6 us
    ppermute x15, waiting for transfers between devices, send(): return lax.ppermute(value, 'orb', [(i, i ^ mask) for i in range(parts)])  20.5 us
    ppermute x15, starting transfers between devices, send(): return lax.ppermute(value, 'orb', [(i, i ^ mask) for i in range(parts)])  19.6 us
    pallas_call x1, Pallas kernels, run_inverse_root(): pl.pallas_call(functools.partial(inverse_root_kernel, masks=masks, side=s...  16.1 us
    pallas_call x2, Pallas kernels, run_margin(): pl.pallas_call(functools.partial(margin_kernel, side=side, gain=1.0 / cel...  6.67 us
  transfers between devices with their start and end apart: 21, of which 17 were waited for; matrix products, arithmetic and copies ran while one was open for 0% of the time, Pallas kernels for 21%

profile of v4, /device:TPU:12, one launch (start us, length us, event | category | flops | bytes accessed | tf_op | source)
XLA Modules:
  0.0 292.9 jit_solution(15522750637559265791)
XLA Ops:
  0.6 19.4 %chebyshev.6 = bf16[16,4,8,1024]{3,2,1,0:T(8,128)(2,1)} custom-call(bf16[32,64,1024]{2,1,0:T(8,128)(2,1)} %bitcast.10, f32[64,1024]{1,0:T(8,128)} %pot_ref.7, bf16[256,256]{1,0:T(8,128)(2,1)} %constant.22.kx_ref, bf16[256,256]{1,0:T(8,128)(2,1)} %constant.23.mx_ref, bf16[1024,256]{1,0:T(8,128)(2,1)} %constant.24.kyz_ref, bf16[768,256]{1,0:T(8,128)(2,1)} %constant.25.myz_ref, ...), custom_call_target="tpu_custom_call" | custom-call | flops 13958643712 | bytes 2097152 | tf_op jit(solution)/shard_map/chebyshev/pallas_call | solution.py:136
  20.0 7.2 %all-to-all-start.2 = ((bf16[16,4,8,1024]{3,2,1,0:T(8,128)(2,1)}), bf16[16,4,8,1024]{3,2,1,0:T(8,128)(2,1)S(1)}, u32[]{:S(2)}, u32[]{:S(2)}) async-start(bf16[16,4,8,1024]{3,2,1,0:T(8,128)(2,1)} %chebyshev.6), calls=%async_computation.2 | async-start | bytes 2097152 | tf_op jit(solution)/shard_map/all_to_all | solution.py:439
  27.2 19.4 %chebyshev.5 = bf16[16,4,8,1024]{3,2,1,0:T(8,128)(2,1)} custom-call(bf16[32,64,1024]{2,1,0:T(8,128)(2,1)} %bitcast.11, f32[64,1024]{1,0:T(8,128)} %pot_ref.7, bf16[256,256]{1,0:T(8,128)(2,1)} %constant.22.kx_ref, bf16[256,256]{1,0:T(8,128)(2,1)} %constant.23.mx_ref, bf16[1024,256]{1,0:T(8,128)(2,1)} %constant.24.kyz_ref, bf16[768,256]{1,0:T(8,128)(2,1)} %constant.25.myz_ref, ...), custom_call_target="tpu_custom_call" | custom-call | flops 13958643712 | bytes 2097152 | tf_op jit(solution)/shard_map/chebyshev/pallas_call | solution.py:136
  46.5 6.0 %all-to-all-done.2.refs_2_.refs_3_ = bf16[16,4,8,1024]{3,2,1,0:T(8,128)(2,1)S(1)} async-done(((bf16[16,4,8,1024]{3,2,1,0:T(8,128)(2,1)}), bf16[16,4,8,1024]{3,2,1,0:T(8,128)(2,1)S(1)}, u32[]{:S(2)}, u32[]{:S(2)}) %all-to-all-start.2) | async-done | bytes 1048608 | tf_op jit(solution)/shard_map/all_to_all | solution.py:439
  52.5 4.9 %all-to-all-start.1 = ((bf16[16,4,8,1024]{3,2,1,0:T(8,128)(2,1)}), bf16[16,4,8,1024]{3,2,1,0:T(8,128)(2,1)S(1)}, u32[]{:S(2)}, u32[]{:S(2)}) async-start(bf16[16,4,8,1024]{3,2,1,0:T(8,128)(2,1)} %chebyshev.5), calls=%async_computation.1 | async-start | bytes 2097152 | tf_op jit(solution)/shard_map/all_to_all | solution.py:439
  57.4 19.4 %chebyshev.4 = bf16[16,4,8,1024]{3,2,1,0:T(8,128)(2,1)} custom-call(bf16[32,64,1024]{2,1,0:T(8,128)(2,1)} %bitcast.12, f32[64,1024]{1,0:T(8,128)} %pot_ref.7, bf16[256,256]{1,0:T(8,128)(2,1)} %constant.22.kx_ref, bf16[256,256]{1,0:T(8,128)(2,1)} %constant.23.mx_ref, bf16[1024,256]{1,0:T(8,128)(2,1)} %constant.24.kyz_ref, bf16[768,256]{1,0:T(8,128)(2,1)} %constant.25.myz_ref, ...), custom_call_target="tpu_custom_call" | custom-call | flops 13958643712 | bytes 2097152 | tf_op jit(solution)/shard_map/chebyshev/pallas_call | solution.py:136
  76.8 4.6 %all-to-all-done.1.refs_1_.refs_2_ = bf16[16,4,8,1024]{3,2,1,0:T(8,128)(2,1)S(1)} async-done(((bf16[16,4,8,1024]{3,2,1,0:T(8,128)(2,1)}), bf16[16,4,8,1024]{3,2,1,0:T(8,128)(2,1)S(1)}, u32[]{:S(2)}, u32[]{:S(2)}) %all-to-all-start.1) | async-done | bytes 1048608 | tf_op jit(solution)/shard_map/all_to_all | solution.py:439
  81.3 5.1 %all-to-all-start = ((bf16[16,4,8,1024]{3,2,1,0:T(8,128)(2,1)}), bf16[16,4,8,1024]{3,2,1,0:T(8,128)(2,1)S(1)}, u32[]{:S(2)}, u32[]{:S(2)}) async-start(bf16[16,4,8,1024]{3,2,1,0:T(8,128)(2,1)} %chebyshev.4), calls=%async_computation | async-start | bytes 2097152 | tf_op jit(solution)/shard_map/all_to_all | solution.py:439
  86.4 19.4 %chebyshev.7 = bf16[16,4,8,1024]{3,2,1,0:T(8,128)(2,1)} custom-call(bf16[32,64,1024]{2,1,0:T(8,128)(2,1)} %bitcast.13, f32[64,1024]{1,0:T(8,128)} %pot_ref.7, bf16[256,256]{1,0:T(8,128)(2,1)} %constant.22.kx_ref, bf16[256,256]{1,0:T(8,128)(2,1)} %constant.23.mx_ref, bf16[1024,256]{1,0:T(8,128)(2,1)} %constant.24.kyz_ref, bf16[768,256]{1,0:T(8,128)(2,1)} %constant.25.myz_ref, ...), custom_call_target="tpu_custom_call" | custom-call | flops 13958643712 | bytes 2097152 | tf_op jit(solution)/shard_map/chebyshev/pallas_call | solution.py:136
  105.8 4.5 %all-to-all-done.refs_0_.refs_1_ = bf16[16,4,8,1024]{3,2,1,0:T(8,128)(2,1)S(1)} async-done(((bf16[16,4,8,1024]{3,2,1,0:T(8,128)(2,1)}), bf16[16,4,8,1024]{3,2,1,0:T(8,128)(2,1)S(1)}, u32[]{:S(2)}, u32[]{:S(2)}) %all-to-all-start) | async-done | bytes 1048608 | tf_op jit(solution)/shard_map/all_to_all | solution.py:439
  110.3 5.1 %all-to-all-start.3 = ((bf16[16,4,8,1024]{3,2,1,0:T(8,128)(2,1)}), bf16[16,4,8,1024]{3,2,1,0:T(8,128)(2,1)}, u32[]{:S(2)}, u32[]{:S(2)}) async-start(bf16[16,4,8,1024]{3,2,1,0:T(8,128)(2,1)} %chebyshev.7), calls=%async_computation.3 | async-start | bytes 2097152 | tf_op jit(solution)/shard_map/all_to_all | solution.py:439
  115.3 3.0 %margin.2 = f32[16,48,128]{2,1,0:T(8,128)S(1)} custom-call(s32[1]{0:T(128)} %bitcast.me_ref, bf16[16,4,8,1024]{3,2,1,0:T(8,128)(2,1)S(1)} %all-to-all-done.refs_0_.refs_1_, bf16[16,4,8,1024]{3,2,1,0:T(8,128)(2,1)S(1)} %all-to-all-done.1.refs_1_.refs_2_, bf16[16,4,8,1024]{3,2,1,0:T(8,128)(2,1)S(1)} %all-to-all-done.2.refs_2_.refs_3_), custom_call_target="tpu_custom_call" | custom-call | flops 805306368 | bytes 3145728 | tf_op jit(solution)/shard_map/margin/pallas_call | solution.py:215
  118.4 1.5 collective-permute-start
  121.9 2.5 collective-permute-done
  124.4 2.3 collective-permute-done.2
  126.7 1.8 collective-permute-done.1
  128.5 10.8 %all-to-all-done.3.refs_3_.refs_4_ = bf16[16,4,8,1024]{3,2,1,0:T(8,128)(2,1)} async-done(((bf16[16,4,8,1024]{3,2,1,0:T(8,128)(2,1)}), bf16[16,4,8,1024]{3,2,1,0:T(8,128)(2,1)}, u32[]{:S(2)}, u32[]{:S(2)}) %all-to-all-start.3) | async-done | bytes 1048608 | tf_op jit(solution)/shard_map/all_to_all | solution.py:439
  139.3 3.7 %margin.3 = f32[16,32,128]{2,1,0:T(8,128)S(1)} custom-call(s32[1]{0:T(128)} %bitcast.me_ref, bf16[16,4,8,1024]{3,2,1,0:T(8,128)(2,1)S(1)} %all-to-all-done.refs_0_.refs_1_, bf16[16,4,8,1024]{3,2,1,0:T(8,128)(2,1)S(1)} %all-to-all-done.1.refs_1_.refs_2_, bf16[16,4,8,1024]{3,2,1,0:T(8,128)(2,1)S(1)} %all-to-all-done.2.refs_2_.refs_3_, ...), custom_call_target="tpu_custom_call" | custom-call | flops 536870912 | bytes 4194304 | tf_op jit(solution)/shard_map/margin/pallas_call | solution.py:215
  143.7 1.6 collective-permute-start.5
  147.3 1.5 collective-permute-done.5
  149.7 1.8 collective-permute-start.8
  151.5 2.6 collective-permute-start.7
  154.1 2.5 collective-permute-done.7
  157.2 3.9 %collective-permute-start.10 = (f32[1,80,128]{2,1,0:T(8,128)S(1)}, f32[1,80,128]{2,1,0:T(8,128)S(1)}, u32[]{:S(2)}, u32[]{:S(2)}) collective-permute-start(f32[1,80,128]{2,1,0:T(8,128)S(1)} %get-tuple-element.7), channel_id=1, source_target_pairs={{0,8},{1,9},{2,10},{3,11},{4,12},{5,13},{6,14},{7,15},{8,0},{9,1},... | collective-permute-start | bytes 122888 | tf_op jit(solution)/shard_map/ppermute | solution.py:256
  161.1 2.4 collective-permute-done.10
  163.5 1.6 collective-permute-done.9
  168.7 4.3 %collective-permute-done.12 = f32[4,80,128]{2,1,0:T(8,128)S(1)} collective-permute-done((f32[4,80,128]{2,1,0:T(8,128)S(1)}, f32[4,80,128]{2,1,0:T(8,128)S(1)}, u32[]{:S(2)}, u32[]{:S(2)}) %collective-permute-start.12) | collective-permute-done | bytes 163872 | tf_op jit(solution)/shard_map/ppermute | solution.py:256
  173.2 16.1 %inverse_root.1.refs_0_ = bf16[512,512]{1,0:T(8,128)(2,1)S(1)} custom-call(s32[1]{0:T(128)} %bitcast.me_ref, f32[16,80,128]{2,1,0:T(8,128)S(1)} %constant_dynamic-update-slice_fusion.held_ref), custom_call_target="tpu_custom_call" | custom-call | flops 13690208256 | bytes 1048576 | tf_op jit(solution)/shard_map/inverse_root/pallas_call | solution.py:337
  189.3 5.6 %rotate.1 = (bf16[16,4,4,8,1024]{4,3,2,1,0:T(8,128)(2,1)}, f32[4,1,1024]{2,1,0:T(1,128)S(1)}) custom-call(bf16[512,512]{1,0:T(8,128)(2,1)S(1)} %inverse_root.1.refs_0_, bf16[16,4,8,1024]{3,2,1,0:T(8,128)(2,1)S(1)} %all-to-all-done.refs_0_.refs_1_, bf16[16,4,8,1024]{3,2,1,0:T(8,128)(2,1)S(1)} %all-to-all-done.1.refs_1_.refs_2_, ...), custom_call_target="tpu_custom_call" | custom-call | flops 2147483648 | bytes 8388608 | tf_op jit(solution)/shard_map/rotate/pallas_call | solution.py:378
  195.0 5.3 %all-to-all-start.4 = ((bf16[16,4,4,8,1024]{4,3,2,1,0:T(8,128)(2,1)}), bf16[16,4,4,8,1024]{4,3,2,1,0:T(8,128)(2,1)}, u32[]{:S(2)}, u32[]{:S(2)}) async-start(bf16[16,4,4,8,1024]{4,3,2,1,0:T(8,128)(2,1)} %get-tuple-element.4), calls=%async_computation.4 | async-start | bytes 8388608 | tf_op jit(solution)/shard_map/all_to_all | solution.py:439
  202.2 85.0 %all-to-all-done.4.refs_0_ = bf16[16,4,4,8,1024]{4,3,2,1,0:T(8,128)(2,1)} async-done(((bf16[16,4,4,8,1024]{4,3,2,1,0:T(8,128)(2,1)}), bf16[16,4,4,8,1024]{4,3,2,1,0:T(8,128)(2,1)}, u32[]{:S(2)}, u32[]{:S(2)}) %all-to-all-start.4) | async-done | bytes 4194336 | tf_op jit(solution)/shard_map/all_to_all | solution.py:439
  287.2 5.8 %restore.1 = bf16[32,64,1024]{2,1,0:T(8,128)(2,1)} custom-call(bf16[16,4,4,8,1024]{4,3,2,1,0:T(8,128)(2,1)} %all-to-all-done.4.refs_0_), custom_call_target="tpu_custom_call" | custom-call | bytes 8388608 | tf_op jit(solution)/shard_map/restore/pallas_call | solution.py:415
  (34 shorter events, 11.8 us)
Async XLA Ops:
  20.0 32.5 %all-to-all-start.2 = ((bf16[16,4,8,1024]{3,2,1,0:T(8,128)(2,1)}), bf16[16,4,8,1024]{3,2,1,0:T(8,128)(2,1)S(1)}, u32[]{:S(2)}, u32[]{:S(2)}) async-start(bf16[16,4,8,1024]{3,2,1,0:T(8,128)(2,1)} %chebyshev.6), calls=%async_computation.2 | async-start | bytes 2097152 | tf_op jit(solution)/shard_map/all_to_all | solution.py:439
  52.5 28.9 %all-to-all-start.1 = ((bf16[16,4,8,1024]{3,2,1,0:T(8,128)(2,1)}), bf16[16,4,8,1024]{3,2,1,0:T(8,128)(2,1)S(1)}, u32[]{:S(2)}, u32[]{:S(2)}) async-start(bf16[16,4,8,1024]{3,2,1,0:T(8,128)(2,1)} %chebyshev.5), calls=%async_computation.1 | async-start | bytes 2097152 | tf_op jit(solution)/shard_map/all_to_all | solution.py:439
  81.3 28.9 %all-to-all-start = ((bf16[16,4,8,1024]{3,2,1,0:T(8,128)(2,1)}), bf16[16,4,8,1024]{3,2,1,0:T(8,128)(2,1)S(1)}, u32[]{:S(2)}, u32[]{:S(2)}) async-start(bf16[16,4,8,1024]{3,2,1,0:T(8,128)(2,1)} %chebyshev.4), calls=%async_computation | async-start | bytes 2097152 | tf_op jit(solution)/shard_map/all_to_all | solution.py:439
  110.3 29.0 %all-to-all-start.3 = ((bf16[16,4,8,1024]{3,2,1,0:T(8,128)(2,1)}), bf16[16,4,8,1024]{3,2,1,0:T(8,128)(2,1)}, u32[]{:S(2)}, u32[]{:S(2)}) async-start(bf16[16,4,8,1024]{3,2,1,0:T(8,128)(2,1)} %chebyshev.7), calls=%async_computation.3 | async-start | bytes 2097152 | tf_op jit(solution)/shard_map/all_to_all | solution.py:439
  118.4 6.0 %collective-permute-start = (f32[4,48,128]{2,1,0:T(8,128)S(1)}, f32[4,48,128]{2,1,0:T(8,128)S(1)}, u32[]{:S(2)}, u32[]{:S(2)}) collective-permute-start(f32[4,48,128]{2,1,0:T(8,128)S(1)} %get-tuple-element.8), channel_id=1, source_target_pairs={{0,1},{1,0},{2,3},{3,2},{4,5},{5,4},{6,7},{7,6},{8,9},{9,8},{10,11... | collective-permute-start | bytes 294920 | tf_op jit(solution)/shard_map/ppermute | solution.py:256
  119.9 6.8 %collective-permute-start.2 = (f32[4,48,128]{2,1,0:T(8,128)S(1)}, f32[4,48,128]{2,1,0:T(8,128)S(1)}, u32[]{:S(2)}, u32[]{:S(2)}) collective-permute-start(f32[4,48,128]{2,1,0:T(8,128)S(1)} %get-tuple-element.9), channel_id=1, source_target_pairs={{0,3},{1,2},{2,1},{3,0},{4,7},{5,6},{6,5},{7,4},{8,11},{9,10},{10,... | collective-permute-start | bytes 294920 | tf_op jit(solution)/shard_map/ppermute | solution.py:256
  120.5 8.0 %collective-permute-start.1 = (f32[4,48,128]{2,1,0:T(8,128)S(1)}, f32[4,48,128]{2,1,0:T(8,128)S(1)}, u32[]{:S(2)}, u32[]{:S(2)}) collective-permute-start(f32[4,48,128]{2,1,0:T(8,128)S(1)} %get-tuple-element.10), channel_id=1, source_target_pairs={{0,2},{1,3},{2,0},{3,1},{4,6},{5,7},{6,4},{7,5},{8,10},{9,11},{10,... | collective-permute-start | bytes 294920 | tf_op jit(solution)/shard_map/ppermute | solution.py:256
  143.0 4.3 %collective-permute-start.3 = (f32[4,32,128]{2,1,0:T(8,128)S(1)}, f32[4,32,128]{2,1,0:T(8,128)S(1)}, u32[]{:S(2)}, u32[]{:S(2)}) collective-permute-start(f32[4,32,128]{2,1,0:T(8,128)S(1)} %get-tuple-element.11), channel_id=1, source_target_pairs={{0,1},{1,0},{2,3},{3,2},{4,5},{5,4},{6,7},{7,6},{8,9},{9,8},{10,11... | collective-permute-start | bytes 196616 | tf_op jit(solution)/shard_map/ppermute | solution.py:256
  143.7 5.2 %collective-permute-start.5 = (f32[4,32,128]{2,1,0:T(8,128)S(1)}, f32[4,32,128]{2,1,0:T(8,128)S(1)}, u32[]{:S(2)}, u32[]{:S(2)}) collective-permute-start(f32[4,32,128]{2,1,0:T(8,128)S(1)} %get-tuple-element.12), channel_id=1, source_target_pairs={{0,3},{1,2},{2,1},{3,0},{4,7},{5,6},{6,5},{7,4},{8,11},{9,10},{10,... | collective-permute-start | bytes 196616 | tf_op jit(solution)/shard_map/ppermute | solution.py:256
  145.3 4.3 %collective-permute-start.4 = (f32[4,32,128]{2,1,0:T(8,128)S(1)}, f32[4,32,128]{2,1,0:T(8,128)S(1)}, u32[]{:S(2)}, u32[]{:S(2)}) collective-permute-start(f32[4,32,128]{2,1,0:T(8,128)S(1)} %get-tuple-element.13), channel_id=1, source_target_pairs={{0,2},{1,3},{2,0},{3,1},{4,6},{5,7},{6,4},{7,5},{8,10},{9,11},{10,... | collective-permute-start | bytes 196616 | tf_op jit(solution)/shard_map/ppermute | solution.py:256
  149.6 4.5 %collective-permute-start.6 = (f32[1,80,128]{2,1,0:T(8,128)S(1)}, f32[1,80,128]{2,1,0:T(8,128)S(1)}, u32[]{:S(2)}, u32[]{:S(2)}) collective-permute-start(f32[1,80,128]{2,1,0:T(8,128)S(1)} %get-tuple-element.14), channel_id=1, source_target_pairs={{0,4},{1,5},{2,6},{3,7},{4,0},{5,1},{6,2},{7,3},{8,12},{9,13},{10,... | collective-permute-start | bytes 122888 | tf_op jit(solution)/shard_map/ppermute | solution.py:256
  149.7 4.4 %collective-permute-start.8 = (f32[1,80,128]{2,1,0:T(8,128)S(1)}, f32[1,80,128]{2,1,0:T(8,128)S(1)}, u32[]{:S(2)}, u32[]{:S(2)}) collective-permute-start(f32[1,80,128]{2,1,0:T(8,128)S(1)} %get-tuple-element.15), channel_id=1, source_target_pairs={{0,12},{1,13},{2,14},{3,15},{4,8},{5,9},{6,10},{7,11},{8,4},{9,5},... | collective-permute-start | bytes 122888 | tf_op jit(solution)/shard_map/ppermute | solution.py:256
  151.5 5.1 %collective-permute-start.7 = (f32[1,80,128]{2,1,0:T(8,128)S(1)}, f32[1,80,128]{2,1,0:T(8,128)S(1)}, u32[]{:S(2)}, u32[]{:S(2)}) collective-permute-start(f32[1,80,128]{2,1,0:T(8,128)S(1)} %get-tuple-element.16), channel_id=1, source_target_pairs={{0,8},{1,9},{2,10},{3,11},{4,12},{5,13},{6,14},{7,15},{8,0},{9,1},... | collective-permute-start | bytes 122888 | tf_op jit(solution)/shard_map/ppermute | solution.py:256
  156.6 4.5 %collective-permute-start.11 = (f32[1,80,128]{2,1,0:T(8,128)S(1)}, f32[1,80,128]{2,1,0:T(8,128)S(1)}, u32[]{:S(2)}, u32[]{:S(2)}) collective-permute-start(f32[1,80,128]{2,1,0:T(8,128)S(1)} %get-tuple-element.7), channel_id=1, source_target_pairs={{0,12},{1,13},{2,14},{3,15},{4,8},{5,9},{6,10},{7,11},{8,4},{9,5},... | collective-permute-start | bytes 122888 | tf_op jit(solution)/shard_map/ppermute | solution.py:256
  157.2 6.3 %collective-permute-start.10 = (f32[1,80,128]{2,1,0:T(8,128)S(1)}, f32[1,80,128]{2,1,0:T(8,128)S(1)}, u32[]{:S(2)}, u32[]{:S(2)}) collective-permute-start(f32[1,80,128]{2,1,0:T(8,128)S(1)} %get-tuple-element.7), channel_id=1, source_target_pairs={{0,8},{1,9},{2,10},{3,11},{4,12},{5,13},{6,14},{7,15},{8,0},{9,1},... | collective-permute-start | bytes 122888 | tf_op jit(solution)/shard_map/ppermute | solution.py:256
  161.1 4.0 %collective-permute-start.9 = (f32[1,80,128]{2,1,0:T(8,128)S(1)}, f32[1,80,128]{2,1,0:T(8,128)S(1)}, u32[]{:S(2)}, u32[]{:S(2)}) collective-permute-start(f32[1,80,128]{2,1,0:T(8,128)S(1)} %get-tuple-element.7), channel_id=1, source_target_pairs={{0,4},{1,5},{2,6},{3,7},{4,0},{5,1},{6,2},{7,3},{8,12},{9,13},{10,... | collective-permute-start | bytes 122888 | tf_op jit(solution)/shard_map/ppermute | solution.py:256
  165.1 8.1 %collective-permute-start.14 = (f32[4,80,128]{2,1,0:T(8,128)S(1)}, f32[4,80,128]{2,1,0:T(8,128)S(1)}, u32[]{:S(2)}, u32[]{:S(2)}) collective-permute-start(f32[4,80,128]{2,1,0:T(8,128)S(1)} %pad_maximum_fusion), channel_id=1, source_target_pairs={{0,3},{1,2},{2,1},{3,0},{4,7},{5,6},{6,5},{7,4},{8,11},{9,10},{10,... | collective-permute-start | bytes 491528 | tf_op jit(solution)/shard_map/ppermute | solution.py:256
  166.5 6.6 %collective-permute-start.13 = (f32[4,80,128]{2,1,0:T(8,128)S(1)}, f32[4,80,128]{2,1,0:T(8,128)S(1)}, u32[]{:S(2)}, u32[]{:S(2)}) collective-permute-start(f32[4,80,128]{2,1,0:T(8,128)S(1)} %pad_maximum_fusion), channel_id=1, source_target_pairs={{0,2},{1,3},{2,0},{3,1},{4,6},{5,7},{6,4},{7,5},{8,10},{9,11},{10,... | collective-permute-start | bytes 491528 | tf_op jit(solution)/shard_map/ppermute | solution.py:256
  167.7 5.3 %collective-permute-start.12 = (f32[4,80,128]{2,1,0:T(8,128)S(1)}, f32[4,80,128]{2,1,0:T(8,128)S(1)}, u32[]{:S(2)}, u32[]{:S(2)}) collective-permute-start(f32[4,80,128]{2,1,0:T(8,128)S(1)} %pad_maximum_fusion), channel_id=1, source_target_pairs={{0,1},{1,0},{2,3},{3,2},{4,5},{5,4},{6,7},{7,6},{8,9},{9,8},{10,11... | collective-permute-start | bytes 491528 | tf_op jit(solution)/shard_map/ppermute | solution.py:256
  195.0 92.2 %all-to-all-start.4 = ((bf16[16,4,4,8,1024]{4,3,2,1,0:T(8,128)(2,1)}), bf16[16,4,4,8,1024]{4,3,2,1,0:T(8,128)(2,1)}, u32[]{:S(2)}, u32[]{:S(2)}) async-start(bf16[16,4,4,8,1024]{4,3,2,1,0:T(8,128)(2,1)} %get-tuple-element.4), calls=%async_computation.4 | async-start | bytes 8388608 | tf_op jit(solution)/shard_map/all_to_all | solution.py:439
  200.3 1.2 collective-permute-start.15
